TPU v7x, 32 devices: a whole 2x2x4 slice. The times are simulated.
32 devices in a mesh: chan: 16 (over z, x, core), tm: 2 (over y).
Axes of the slice: x: 2, y: 2, z: 4, core: 2. Of those that a mesh axis runs over, the one named last changes fastest.
Arguments:
- volt: bfloat16 [2, 64, 2048, 512], P(None, None, ('chan', 'tm')), may hold values from -40 to 40
- windows: int32 [64, 2], P('chan'), may hold values from 0 to 2048, as said below
- start_basis: float32 [2, 64, 8, 512], P(None, 'chan'), may hold values from -6 to 6
- positions: float32 [2, 512], replicated, may hold values from -16 to 16
- pointing: float32 [2, 1024], replicated, may hold values from -0.7 to 0.7
- beam_dir: int32 [1024], replicated, may hold values from 0 to 1023, each once
Outputs:
- power: float32 [64, 1024], P('chan', 'tm')
Inputs may be any that keep to these rules, and one draw needn't show every extreme that they name: `windows`: each row holds a channel's first window sample and one past its last; every window holds 1024 samples or more. `beam_dir`: each table entry is named by exactly one beam.
All inputs are finite; a program needn't handle non-finite values.
Results may differ from a plain program's by a relative error of at most 0.0024.
Values may be sent and summed in bfloat16 or wider, within the bound.
No kernel may reach another device: no remote copies, remote signals or barrier semaphores. Data moves between devices by JAX's collectives and lax.ppermute only.
A program may use at most 128 MiB of HBM per device.

v0:
```python
import math

import jax
import jax.numpy as jnp
from jax import lax
from jax.sharding import PartitionSpec as P

ITERS = 6


EPS = 1e-06
TWO_PI = 2.0 * math.pi


def orthonormal(real_part, imag_part):
    number = real_part.shape[-2]
    base_real = []
    base_imag = []
    for column in range(number):
        vec_real = real_part[..., column, :]
        vec_imag = imag_part[..., column, :]
        for earlier in range(column):
            prev_real = base_real[earlier]
            prev_imag = base_imag[earlier]
            coef_real = jnp.sum(prev_real * vec_real + prev_imag * vec_imag, axis=-1, keepdims=True)
            coef_imag = jnp.sum(prev_real * vec_imag - prev_imag * vec_real, axis=-1, keepdims=True)
            vec_real = vec_real - (coef_real * prev_real - coef_imag * prev_imag)
            vec_imag = vec_imag - (coef_real * prev_imag + coef_imag * prev_real)
        inverse = lax.rsqrt(
            jnp.sum(vec_real * vec_real + vec_imag * vec_imag, axis=-1, keepdims=True) + EPS
        )
        base_real.append(vec_real * inverse)
        base_imag.append(vec_imag * inverse)
    return (jnp.stack(base_real, axis=-2), jnp.stack(base_imag, axis=-2))


def fdot(left, right):
    return jnp.dot(left, right, preferred_element_type=jnp.float32)


def fsum(form, left, right):
    return jnp.einsum(form, left, right, preferred_element_type=jnp.float32)


def channel_power(volt_real, volt_imag, base_real, base_imag, freq, direction, positions):
    low_real = base_real.astype(jnp.bfloat16)
    low_imag = base_imag.astype(jnp.bfloat16)
    full_real = (fdot(volt_real, low_real.T) + fdot(volt_imag, low_imag.T)).astype(jnp.bfloat16)
    full_imag = (fdot(volt_imag, low_real.T) - fdot(volt_real, low_imag.T)).astype(jnp.bfloat16)
    removed_real = fdot(full_real, low_real) - fdot(full_imag, low_imag)
    removed_imag = fdot(full_real, low_imag) + fdot(full_imag, low_real)
    clean_real = (volt_real.astype(jnp.float32) - removed_real).astype(jnp.bfloat16)
    clean_imag = (volt_imag.astype(jnp.float32) - removed_imag).astype(jnp.bfloat16)
    phase = (
        TWO_PI
        * freq
        * (
            positions[0][:, None] * direction[0][None, :]
            + positions[1][:, None] * direction[1][None, :]
        )
    )
    steer_real = jnp.cos(phase).astype(jnp.bfloat16)
    steer_imag = jnp.sin(phase).astype(jnp.bfloat16)
    beam_real = fdot(clean_real, steer_real) + fdot(clean_imag, steer_imag)
    beam_imag = fdot(clean_imag, steer_real) - fdot(clean_real, steer_imag)
    return jnp.sum(beam_real * beam_real + beam_imag * beam_imag, axis=0)


def body(volt, windows, start_basis, positions, pointing, beam_dir):
    parts, channels_all, rows_in, stations = volt.shape
    n_chan = lax.axis_size("chan")
    n_time = lax.axis_size("tm")
    chan_dev = channels_all // n_chan
    chan_at = lax.axis_index("chan")
    time_at = lax.axis_index("tm")
    total_time = rows_in * n_chan * n_time
    per_device = chan_dev // n_time
    blocks = volt.reshape(parts, n_chan * n_time, per_device, rows_in, stations)
    moved = lax.all_to_all(blocks, ("chan", "tm"), split_axis=1, concat_axis=3, tiled=True)
    local = moved.reshape(parts, per_device, total_time, stations)
    sample_at = jnp.arange(total_time, dtype=jnp.int32)
    first_channel = chan_at * chan_dev + time_at * per_device
    own_windows = lax.dynamic_slice_in_dim(windows, time_at * per_device, per_device, 0)
    own_basis = lax.dynamic_slice_in_dim(start_basis, time_at * per_device, per_device, 1)
    volt_real = local[0]
    volt_imag = local[1]
    window_mask = (
        (sample_at[None, :] >= own_windows[:, 0:1]) & (sample_at[None, :] < own_windows[:, 1:2])
    ).astype(jnp.float32)
    base_real, base_imag = orthonormal(own_basis[0], own_basis[1])
    for iteration in range(ITERS):
        low_real = base_real.astype(jnp.bfloat16)
        low_imag = base_imag.astype(jnp.bfloat16)
        proj_real = fsum("cts,cks->ctk", volt_real, low_real) + fsum(
            "cts,cks->ctk", volt_imag, low_imag
        )
        proj_imag = fsum("cts,cks->ctk", volt_imag, low_real) - fsum(
            "cts,cks->ctk", volt_real, low_imag
        )
        proj_real = (proj_real * window_mask[:, :, None]).astype(jnp.bfloat16)
        proj_imag = (proj_imag * window_mask[:, :, None]).astype(jnp.bfloat16)
        image_real = fsum("ctk,cts->cks", proj_real, volt_real) - fsum(
            "ctk,cts->cks", proj_imag, volt_imag
        )
        image_imag = fsum("ctk,cts->cks", proj_real, volt_imag) + fsum(
            "ctk,cts->cks", proj_imag, volt_real
        )
        base_real, base_imag = orthonormal(image_real, image_imag)
    direction = jnp.take(pointing, beam_dir, axis=1)
    channel_ids = first_channel + jnp.arange(volt_real.shape[0], dtype=jnp.int32)

    def one_channel(inputs):
        chan_real, chan_imag, basis_re, basis_im, channel = inputs
        freq = 1.0 + channel.astype(jnp.float32) / channels_all
        return channel_power(chan_real, chan_imag, basis_re, basis_im, freq, direction, positions)

    partial_power = lax.map(one_channel, (volt_real, volt_imag, base_real, base_imag, channel_ids))
    scaled = partial_power / (total_time * stations)
    return lax.all_to_all(scaled, "tm", split_axis=1, concat_axis=0, tiled=True)


def solution(mesh):
    return jax.shard_map(
        body,
        mesh=mesh,
        in_specs=(
            P(None, None, ("chan", "tm"), None),
            P("chan", None),
            P(None, "chan", None, None),
            P(),
            P(),
            P(),
        ),
        out_specs=P("chan", "tm"),
        check_vma=False,
    )
```

profile of v0, /device:TPU:0, one launch (start us, length us, event | category | flops | bytes accessed | tf_op | source)
XLA Modules:
  0.0 407.3 jit_solution(8869985679007207590)
XLA Ops:
  0.0 7.7 %copy.2137 = bf16[2,32,2,64,512]{4,3,2,0,1:T(8,128)(2,1)} copy(bf16[2,32,2,64,512]{4,3,2,1,0:T(8,128)(2,1)} %bitcast.1410) | data formatting | bytes 16777216 | tf_op jit(solution)/shard_map/reshape | solution.py:78
  7.7 7.5 %all-to-all-start = ((bf16[2,32,2,64,512]{4,3,2,0,1:T(8,128)(2,1)}), bf16[2,32,2,64,512]{4,3,2,0,1:T(8,128)(2,1)}, u32[]{:S(2)}, u32[]{:S(2)}) async-start(bf16[2,32,2,64,512]{4,3,2,0,1:T(8,128)(2,1)} %copy.2137), calls=%async_computation | async-start | bytes 16777216 | tf_op jit(solution)/shard_map/all_to_all | solution.py:79
  15.5 2.8 gather_fusion
  24.0 177.3 %all-to-all-done = bf16[2,32,2,64,512]{4,3,2,0,1:T(8,128)(2,1)} async-done(((bf16[2,32,2,64,512]{4,3,2,0,1:T(8,128)(2,1)}), bf16[2,32,2,64,512]{4,3,2,0,1:T(8,128)(2,1)}, u32[]{:S(2)}, u32[]{:S(2)}) %all-to-all-start) | async-done | bytes 8388640 | tf_op jit(solution)/shard_map/all_to_all | solution.py:79
  201.3 4.2 %fusion.294 = (bf16[1,1,2,32,64,512]{5,4,2,0,3,1:T(8,128)(2,1)S(1)}, bf16[1,1,2,32,64,512]{5,4,2,0,3,1:T(8,128)(2,1)S(1)}) fusion(bf16[2,1,2,32,64,512]{5,4,2,0,3,1:T(8,128)(2,1)} %bitcast.12), kind=kLoop, calls=%fused_computation.1637 | loop fusion | bytes 16777216 | tf_op jit(solution)/shard_map/slice | solution.py:86
  207.6 1.2 fusion.34
  231.5 1.6 fusion.65
  258.1 1.4 fusion.42
  282.2 117.9 %while.10 = (s32[]{:T(128)}, f32[2,1024]{1,0:T(2,128)S(1)}, bf16[2,2048,512]{2,1,0:T(8,128)(2,1)}, bf16[2,8,512]{2,0,1:T(2,128)(2,1)S(1)}, bf16[2,2048,512]{2,1,...) while((s32[]{:T(128)}, f32[2,1024]{1,0:T(2,128)S(1)}, ...), condition=%wide.region_450.451_spmd, body=%wide.region_448.0_spmd.sunk | while | flops 8755674112 | bytes 126480664 | solution.py:117
  306.2 2.2 fusion.463
  308.5 2.2 fusion.464
  310.7 2.4 fusion.460
  316.8 8.5 %fusion.470 = f32[2048,1024]{1,0:T(8,128)S(1)} fusion(bf16[2048,512]{1,0:T(8,128)(2,1)S(1)} %subtract_convert_fusion.4, f32[1024]{0:T(1024)S(1)} %bitcast.1416, f32[512]{0:T(512)S(1)} %bitcast.1424, f32[1024]{0:T(1024)S(1)} %bitcast.1412, f32[512]{0:T(512)S(1)} %bitcast.1420, f32[]{:T(128)} %bitcast.1358), kind=kOutput, calls=%fused_computation.23.clone.1 | convolution fusion | flops 2150105088 | bytes 10498052 | tf_op jit(solution)/shard_map/while/body/eval_jaxpr/dot_general | solution.py:38
  325.3 8.4 %fusion.467 = f32[2048,1024]{1,0:T(8,128)S(1)} fusion(bf16[2048,512]{1,0:T(8,128)(2,1)S(1)} %subtract_convert_fusion.4, f32[1024]{0:T(1024)S(1)} %bitcast.1417, f32[512]{0:T(512)S(1)} %bitcast.1425, f32[1024]{0:T(1024)S(1)} %bitcast.1413, f32[512]{0:T(512)S(1)} %bitcast.1421, f32[]{:T(128)} %bitcast.1358), kind=kOutput, calls=%fused_computation.21.clone.1 | convolution fusion | flops 2150105088 | bytes 10498052 | tf_op jit(solution)/shard_map/while/body/eval_jaxpr/dot_general | solution.py:38
  333.7 8.4 %fusion.469 = f32[2048,1024]{1,0:T(8,128)S(1)} fusion(bf16[2048,512]{1,0:T(8,128)(2,1)S(1)} %subtract_convert_fusion.5, f32[1024]{0:T(1024)S(1)} %bitcast.1418, f32[512]{0:T(512)S(1)} %bitcast.1426, f32[1024]{0:T(1024)S(1)} %bitcast.1414, f32[512]{0:T(512)S(1)} %bitcast.1422, f32[]{:T(128)} %bitcast.1358), kind=kOutput, calls=%fused_computation.22.clone.1 | convolution fusion | flops 2150105088 | bytes 10498052 | tf_op jit(solution)/shard_map/while/body/eval_jaxpr/dot_general | solution.py:38
  342.1 10.2 %add_reduce_fusion.198 = f32[1024]{0:T(1024)S(1)} fusion(f32[2048,1024]{1,0:T(8,128)S(1)} %fusion.467, f32[2048,1024]{1,0:T(8,128)S(1)} %fusion.469, f32[2048,1024]{1,0:T(8,128)S(1)} %fusion.470, bf16[2048,512]{1,0:T(8,128)(2,1)S(1)} %subtract_convert_fusion.5, f32[1024]{0:T(1024)S(1)} %bitcast.1419, f32[512]{0:T(512)S(1)} %bitcast.1427, ...), kind=kOutput, calls=%fused_computation.1.clone.1 | convolution fusion | flops 2162686976 | bytes 27279364 | tf_op jit(solution)/shard_map/while/body/eval_jaxpr/dot_general | solution.py:38
  353.9 2.2 fusion.463
  356.1 2.2 fusion.464
  358.4 2.4 fusion.460
  364.5 8.5 %fusion.470 = f32[2048,1024]{1,0:T(8,128)S(1)} fusion(bf16[2048,512]{1,0:T(8,128)(2,1)S(1)} %subtract_convert_fusion.4, f32[1024]{0:T(1024)S(1)} %bitcast.1416, f32[512]{0:T(512)S(1)} %bitcast.1424, f32[1024]{0:T(1024)S(1)} %bitcast.1412, f32[512]{0:T(512)S(1)} %bitcast.1420, f32[]{:T(128)} %bitcast.1358), kind=kOutput, calls=%fused_computation.23.clone.1 | convolution fusion | flops 2150105088 | bytes 10498052 | tf_op jit(solution)/shard_map/while/body/eval_jaxpr/dot_general | solution.py:38
  373.0 8.4 %fusion.467 = f32[2048,1024]{1,0:T(8,128)S(1)} fusion(bf16[2048,512]{1,0:T(8,128)(2,1)S(1)} %subtract_convert_fusion.4, f32[1024]{0:T(1024)S(1)} %bitcast.1417, f32[512]{0:T(512)S(1)} %bitcast.1425, f32[1024]{0:T(1024)S(1)} %bitcast.1413, f32[512]{0:T(512)S(1)} %bitcast.1421, f32[]{:T(128)} %bitcast.1358), kind=kOutput, calls=%fused_computation.21.clone.1 | convolution fusion | flops 2150105088 | bytes 10498052 | tf_op jit(solution)/shard_map/while/body/eval_jaxpr/dot_general | solution.py:38
  381.4 8.4 %fusion.469 = f32[2048,1024]{1,0:T(8,128)S(1)} fusion(bf16[2048,512]{1,0:T(8,128)(2,1)S(1)} %subtract_convert_fusion.5, f32[1024]{0:T(1024)S(1)} %bitcast.1418, f32[512]{0:T(512)S(1)} %bitcast.1426, f32[1024]{0:T(1024)S(1)} %bitcast.1414, f32[512]{0:T(512)S(1)} %bitcast.1422, f32[]{:T(128)} %bitcast.1358), kind=kOutput, calls=%fused_computation.22.clone.1 | convolution fusion | flops 2150105088 | bytes 10498052 | tf_op jit(solution)/shard_map/while/body/eval_jaxpr/dot_general | solution.py:38
  389.8 10.2 %add_reduce_fusion.198 = f32[1024]{0:T(1024)S(1)} fusion(f32[2048,1024]{1,0:T(8,128)S(1)} %fusion.467, f32[2048,1024]{1,0:T(8,128)S(1)} %fusion.469, f32[2048,1024]{1,0:T(8,128)S(1)} %fusion.470, bf16[2048,512]{1,0:T(8,128)(2,1)S(1)} %subtract_convert_fusion.5, f32[1024]{0:T(1024)S(1)} %bitcast.1419, f32[512]{0:T(512)S(1)} %bitcast.1427, ...), kind=kOutput, calls=%fused_computation.1.clone.1 | convolution fusion | flops 2162686976 | bytes 27279364 | tf_op jit(solution)/shard_map/while/body/eval_jaxpr/dot_general | solution.py:38
  400.1 6.2 %all_to_all.34 = f32[2,2,512]{2,0,1:T(2,128)S(1)} all-to-all(f32[2,2,512]{2,0,1:T(2,128)S(1)} %bitcast.1428), channel_id=1, replica_groups=mesh['chan'=16,'tm'=2] {'tm'}, dimensions={1} | all-to-all | bytes 16384 | tf_op jit(solution)/shard_map/all_to_all | solution.py:119
  (390 shorter events, 87.2 us)
Async XLA Ops:
  0.0 18.7 %copy-start = (s32[4,2]{0,1:T(2,128)S(1)}, s32[4,2]{0,1:T(2,128)}, u32[]{:S(2)}) copy-start(s32[4,2]{0,1:T(2,128)} %param.9) | copy-start | bytes 100
  7.7 7.5 %copy-start.9 = (f32[2,1024]{1,0:T(2,128)S(1)}, f32[2,1024]{1,0:T(2,128)}, u32[]{:S(2)}) copy-start(f32[2,1024]{1,0:T(2,128)} %param.12) | copy-start | bytes 24580
  7.7 7.7 %copy-start.8 = (s32[1024]{0:T(1024)S(1)}, s32[1024]{0:T(1024)}, u32[]{:S(2)}) copy-start(s32[1024]{0:T(1024)} %param.13) | copy-start | bytes 12292
  7.7 11.1 %copy-start.7 = (f32[2,4,8,512]{3,2,1,0:T(8,128)S(1)}, f32[2,4,8,512]{3,2,1,0:T(8,128)}, u32[]{:S(2)}) copy-start(f32[2,4,8,512]{3,2,1,0:T(8,128)} %param.10) | copy-start | bytes 393220
  7.7 193.5 %all-to-all-start = ((bf16[2,32,2,64,512]{4,3,2,0,1:T(8,128)(2,1)}), bf16[2,32,2,64,512]{4,3,2,0,1:T(8,128)(2,1)}, u32[]{:S(2)}, u32[]{:S(2)}) async-start(bf16[2,32,2,64,512]{4,3,2,0,1:T(8,128)(2,1)} %copy.2137), calls=%async_computation | async-start | bytes 16777216 | tf_op jit(solution)/shard_map/all_to_all | solution.py:79
  205.9 69.8 %copy-start.2 = (bf16[1,1,2,32,64,512]{5,4,3,2,1,0:T(8,128)(2,1)}, bf16[1,1,2,32,64,512]{5,4,3,2,1,0:T(8,128)(2,1)S(1)}, u32[]{:S(2)}) copy-start(bf16[1,1,2,32,64,512]{5,4,3,2,1,0:T(8,128)(2,1)S(1)} %copy.2141) | copy-start | bytes 12582916
  206.4 70.0 %copy-start.4 = (bf16[1,1,2,32,64,512]{5,4,3,2,1,0:T(8,128)(2,1)}, bf16[1,1,2,32,64,512]{5,4,3,2,1,0:T(8,128)(2,1)S(1)}, u32[]{:S(2)}) copy-start(bf16[1,1,2,32,64,512]{5,4,3,2,1,0:T(8,128)(2,1)S(1)} %copy.2138) | copy-start | bytes 12582916
  275.7 6.4 %copy-start.6 = (f32[2,512]{1,0:T(2,128)S(1)}, f32[2,512]{1,0:T(2,128)}, u32[]{:S(2)}) copy-start(f32[2,512]{1,0:T(2,128)} %param.11) | copy-start | bytes 12292
  304.7 8.4 %copy-start.3 = (bf16[2,2048,512]{2,1,0:T(8,128)(2,1)S(1)}, bf16[2,2048,512]{2,1,0:T(8,128)(2,1)}, u32[]{:S(2)}) copy-start(bf16[2,2048,512]{2,1,0:T(8,128)(2,1)} %get-tuple-element.1442) | copy-start | bytes 12582916 | tf_op jit(solution)/shard_map/while
  310.7 3.8 copy-start.5
  352.4 8.4 %copy-start.3 = (bf16[2,2048,512]{2,1,0:T(8,128)(2,1)S(1)}, bf16[2,2048,512]{2,1,0:T(8,128)(2,1)}, u32[]{:S(2)}) copy-start(bf16[2,2048,512]{2,1,0:T(8,128)(2,1)} %get-tuple-element.1442) | copy-start | bytes 12582916 | tf_op jit(solution)/shard_map/while
  358.4 3.8 copy-start.5
  400.1 6.8 %copy-start.1 = (s32[4,2]{0,1:T(2,128)S(1)}, s32[4,2]{0,1:T(2,128)}, u32[]{:S(2)}) copy-start(s32[4,2]{0,1:T(2,128)} %param.9) | copy-start | bytes 100
where the time goes:
time: 411 us; the launch traced here: 407 us
  waiting for transfers between devices  177 us (43%)
  matrix products  137 us (33%)
  other arithmetic  35.5 us (9%)
  loops' own time  24.5 us (6%)
  local copies, waits for them, and re-layouts  18.3 us (4%)
  starting transfers between devices  7.45 us (2%)
  blocking collectives  6.15 us (1%)
    all_to_all x1, waiting for transfers between devices, body(): lax.all_to_all(blocks, ('chan', 'tm'), split_axis=1, concat_axis=3, tiled...  177 us
    dot_general x24, matrix products, fdot(): return jnp.dot(left, right, preferred_element_type=jnp.float32)  92.1 us
    dot_general x48, matrix products, fsum(): return jnp.einsum(form, left, right, preferred_element_type=jnp.float32)  44.9 us
    another operation x1, loops' own time, body(): lax.map(one_channel, (volt_real, volt_imag, base_real, base_imag, channel...  24.5 us
    reduce_sum x56, other arithmetic, orthonormal(): jnp.sum(prev_real * vec_real + prev_imag * vec_imag, axis=-1, keepdims=True)  16.2 us
    reduce_sum x56, other arithmetic, orthonormal(): jnp.sum(vec_real * vec_real + vec_imag * vec_imag, axis=-1, keepdims=True)  10.4 us
  transfers between devices with their start and end apart: 1, of which 1 were waited for; matrix products, arithmetic and copies ran while one was open for 2% of the time, Pallas kernels for 0%

commit v1 on v0

v1 whole, which is shorter than its diff:
```python
import functools

import jax
import jax.numpy as jnp
import numpy as np
from jax import lax
from jax.experimental import pallas as pl
from jax.experimental.pallas import tpu as pltpu
from jax.sharding import Mesh
from jax.sharding import PartitionSpec as P

ITERS = 6
EPS = 1e-06
F32 = jnp.float32
BF16 = jnp.bfloat16
VMEM = pl.BlockSpec(memory_space=pltpu.VMEM)
SMEM = pl.BlockSpec(memory_space=pltpu.SMEM)
VMEM_LIMIT = 40 << 20


def orthonormal(chans):
    number = chans[0][0].shape[0]
    row = lax.broadcasted_iota(jnp.int32, (number, 1), 0)
    for j in range(number):
        after = []
        for re, im in chans:
            top_re, top_im = re[j : j + 1], im[j : j + 1]
            dot_re = jnp.sum(top_re * re + top_im * im, axis=1, keepdims=True)
            dot_im = jnp.sum(top_re * im - top_im * re, axis=1, keepdims=True)
            inverse = lax.rsqrt(dot_re[j : j + 1] + EPS)
            share = jnp.where(row > j, inverse * inverse, 0.0)
            coef_re, coef_im = share * dot_re, share * dot_im
            scale = jnp.where(row == j, inverse, 1.0)
            after.append(
                (
                    re * scale - (coef_re * top_re - coef_im * top_im),
                    im * scale - (coef_re * top_im + coef_im * top_re),
                )
            )
        chans = after
    return chans


def contract(left, right, at_left, at_right):
    return lax.dot_general(
        left, right, (((at_left,), (at_right,)), ((), ())), preferred_element_type=F32
    )


def project(base_re, base_im, volt_re, volt_im):
    first = jnp.concatenate([base_re, -base_im], 0).astype(BF16)
    second = jnp.concatenate([base_im, base_re], 0).astype(BF16)
    return contract(first, volt_re, 1, 1) + contract(second, volt_im, 1, 1)


def split(stacked):
    number = stacked.shape[0] // 2
    return stacked[:number], stacked[number:]


def iterate_kernel(first, win_ref, start_ref, *refs):
    *image_refs, volt_ref, out_ref = refs
    sources, _, channels, rows, stations = volt_ref.shape
    number = out_ref.shape[1] // 2
    total = sources * rows
    chans = []
    for c in range(channels):
        stacked = image_refs[0][c] if first else image_refs[0][c] + image_refs[1][c]
        chans.append(split(stacked))
    chans = orthonormal(chans)
    sample = start_ref[0] + lax.broadcasted_iota(jnp.int32, (1, total), 1)
    for c in range(channels):
        volt_re = volt_ref[:, 0, c].reshape(total, stations)
        volt_im = volt_ref[:, 1, c].reshape(total, stations)
        proj = project(*chans[c], volt_re, volt_im)
        inside = (sample >= win_ref[c, 0]) & (sample < win_ref[c, 1])
        proj = jnp.where(inside, proj, 0.0).astype(BF16)
        by_re = contract(proj, volt_re, 1, 0)
        by_im = contract(proj, volt_im, 1, 0)
        out_ref[c, :number] = by_re[:number] - by_im[number:]
        out_ref[c, number:] = by_im[:number] + by_re[number:]


def iterate(windows, start, images, volt):
    first = len(images) == 1
    channels = images[0].shape[0]
    return pl.pallas_call(
        functools.partial(iterate_kernel, first),
        out_shape=jax.ShapeDtypeStruct(images[0].shape, F32),
        in_specs=[SMEM, SMEM] + [VMEM] * (len(images) + 1),
        out_specs=VMEM,
        compiler_params=pltpu.CompilerParams(vmem_limit_bytes=VMEM_LIMIT),
        cost_estimate=pl.CostEstimate(
            flops=volt.size * 64, bytes_accessed=volt.size * 2, transcendentals=0
        ),
        name="iterate",
    )(windows, start, *images, volt)


def beam_kernel(at, own_ref, other_ref, volt_ref, steer_ref, out_ref, clean_ref):
    sources, _, _, rows, stations = volt_ref.shape
    total = sources * rows

    @pl.when(pl.program_id(0) == 0)
    def _():
        ((base_re, base_im),) = orthonormal([split(own_ref[at] + other_ref[at])])
        volt_re = volt_ref[:, 0, 0].reshape(total, stations)
        volt_im = volt_ref[:, 1, 0].reshape(total, stations)
        full = project(base_re, base_im, volt_re, volt_im).astype(BF16)
        low_re = jnp.concatenate([base_re, -base_im], 0).astype(BF16)
        low_im = jnp.concatenate([base_im, base_re], 0).astype(BF16)
        clean_ref[0] = (volt_re.astype(F32) - contract(full, low_re, 0, 0)).astype(BF16)
        clean_ref[1] = (volt_im.astype(F32) - contract(full, low_im, 0, 0)).astype(BF16)

    clean_re, clean_im = clean_ref[0], clean_ref[1]
    steer_re, steer_im = steer_ref[0, 0], steer_ref[0, 1]
    beam_re = contract(clean_re, steer_re, 1, 0) + contract(clean_im, steer_im, 1, 0)
    beam_im = contract(clean_im, steer_re, 1, 0) - contract(clean_re, steer_im, 1, 0)
    out_ref[0] = jnp.sum(beam_re * beam_re + beam_im * beam_im, axis=0, keepdims=True)


def beam_power(at, images, volt, steer, channel, tile):
    own, other = images
    sources, parts, _, rows, stations = volt.shape
    beams = steer.shape[-1]
    whole = pl.BlockSpec(own.shape, lambda i: (0, 0, 0))
    return pl.pallas_call(
        functools.partial(beam_kernel, at),
        out_shape=jax.ShapeDtypeStruct((1, 1, beams), F32),
        grid=(beams // tile,),
        in_specs=[
            whole,
            whole,
            pl.BlockSpec((sources, parts, 1, rows, stations), lambda i: (0, 0, at, 0, 0)),
            pl.BlockSpec((1, parts, stations, tile), lambda i: (channel, 0, 0, i)),
        ],
        out_specs=pl.BlockSpec((1, 1, tile), lambda i: (0, 0, i)),
        scratch_shapes=[pltpu.VMEM((parts, sources * rows, stations), BF16)],
        compiler_params=pltpu.CompilerParams(vmem_limit_bytes=VMEM_LIMIT),
        cost_estimate=pl.CostEstimate(
            flops=sources * rows * stations * beams * 8,
            bytes_accessed=stations * beams * 4,
            transcendentals=0,
        ),
        name="beams",
    )(own, other, volt, steer)


def turn_series():
    nodes = np.cos((np.arange(4000) + 0.5) / 4000 * np.pi) * 0.25 + 0.25
    angle = 2.0 * np.pi * nodes
    fit = np.polynomial.chebyshev.Chebyshev.fit
    made = []
    for values, degree in ((np.cos(angle), 7), (np.sin(angle) / nodes, 6)):
        series = fit(nodes * nodes, values, degree, domain=[0, 0.25])
        made.append(series.convert(kind=np.polynomial.Polynomial).coef)
    return made


COS_SERIES, SIN_SERIES = turn_series()


def horner(at, series):
    total = jnp.float32(series[-1]) * at + jnp.float32(series[-2])
    for coef in series[-3::-1]:
        total = total * at + jnp.float32(coef)
    return total


def steer_kernel(freq_ref, place_ref, toward_ref, out_ref):
    delay = place_ref[:, 0:1] * toward_ref[0:1, :] + place_ref[:, 1:2] * toward_ref[1:2, :]
    for c in range(out_ref.shape[0]):
        turns = delay * freq_ref[c]
        rest = turns - jnp.round(turns)
        square = rest * rest
        out_ref[c, 0] = horner(square, COS_SERIES).astype(BF16)
        out_ref[c, 1] = (rest * horner(square, SIN_SERIES)).astype(BF16)


def steering(freq, places, toward, tile):
    channels, stations, beams = freq.shape[0], places.shape[0], toward.shape[1]
    return pl.pallas_call(
        steer_kernel,
        out_shape=jax.ShapeDtypeStruct((channels, 2, stations, beams), BF16),
        grid=(beams // tile,),
        in_specs=[
            SMEM,
            pl.BlockSpec((stations, 2), lambda i: (0, 0)),
            pl.BlockSpec((2, tile), lambda i: (0, i)),
        ],
        out_specs=pl.BlockSpec((channels, 2, stations, tile), lambda i: (0, 0, 0, i)),
        compiler_params=pltpu.CompilerParams(vmem_limit_bytes=VMEM_LIMIT),
        cost_estimate=pl.CostEstimate(
            flops=channels * stations * beams * 40,
            bytes_accessed=channels * stations * beams * 4,
            transcendentals=0,
        ),
        name="steering",
    )(freq, places, toward)


SWAP = [(0, 1), (1, 0)]


def body(volt, windows, start_basis, positions, pointing, beam_dir):
    parts, channels_all, rows, stations = volt.shape
    number = start_basis.shape[2]
    n_lo, n_time = lax.axis_size("lo"), lax.axis_size("tm")
    half_at, lo_at, time_at = (lax.axis_index(a) for a in ("hi", "lo", "tm"))
    group = n_lo * n_time
    chan_dev = windows.shape[0]
    per = chan_dev // n_time
    half_time = rows * group
    beams = beam_dir.shape[0]

    blocks = volt.reshape(parts, 2, group, per, rows, stations)
    chunks = [(0, tuple(range(per)))] + [(1, (i,)) for i in range(per)]
    moved = []
    for owner, members in chunks:
        picked = blocks[:, owner, :, members[0] : members[-1] + 1]
        picked = jnp.transpose(picked, (1, 0, 2, 3, 4))
        moved.append(lax.all_to_all(picked, ("lo", "tm"), split_axis=0, concat_axis=0, tiled=True))

    own_windows = lax.dynamic_slice_in_dim(windows, time_at * per, per, 0)
    own_basis = lax.dynamic_slice_in_dim(start_basis, time_at * per, per, 1)
    own_basis = jnp.transpose(own_basis, (1, 0, 2, 3)).reshape(per, parts * number, stations)
    far_windows = lax.ppermute(own_windows, "hi", SWAP)
    far_basis = lax.ppermute(own_basis, "hi", SWAP)
    lower = half_at == 0
    all_windows = [
        jnp.where(lower, own_windows, far_windows),
        jnp.where(lower, far_windows, own_windows),
    ]
    all_basis = [jnp.where(lower, own_basis, far_basis), jnp.where(lower, far_basis, own_basis)]
    first_sample = (half_at * half_time).astype(jnp.int32).reshape(1)

    toward = jnp.take(pointing, beam_dir, axis=1)
    channel_ids = jnp.stack(
        [
            (owner * n_lo + lo_at) * chan_dev + time_at * per + i
            for owner in range(2)
            for i in range(per)
        ]
    )
    freq = 1.0 + channel_ids.astype(F32) / channels_all
    steer = steering(freq, positions.T, toward, 128)

    power = []
    for (owner, members), local in zip(chunks, moved, strict=True):
        pick = slice(members[0], members[-1] + 1)
        win = all_windows[owner][pick]
        images = (all_basis[owner][pick],)
        for _ in range(ITERS):
            image = iterate(win, first_sample, images, local)
            images = (image, lax.ppermute(image, "hi", SWAP))
        for at, member in enumerate(members):
            power.append(beam_power(at, images, local, steer, owner * per + member, min(512, beams)))
    mine = jnp.stack(power).reshape(2, per, n_time, beams // n_time)
    mine = jnp.transpose(mine, (0, 2, 1, 3)) / (2 * half_time * stations)
    flat = mine.reshape(2 * n_time, per, beams // n_time)
    came = lax.all_to_all(flat, ("hi", "tm"), split_axis=0, concat_axis=0, tiled=True)
    came = came.reshape(2, n_time * per, beams // n_time)
    return came[0] + came[1]


def solution(mesh):
    n_chan, n_time = mesh.shape["chan"], mesh.shape["tm"]
    halves = Mesh(mesh.devices.reshape(2, n_chan // 2, n_time), ("hi", "lo", "tm"))
    chan = ("hi", "lo")
    return jax.shard_map(
        body,
        mesh=halves,
        in_specs=(
            P(None, None, ("hi", "lo", "tm"), None),
            P(chan, None),
            P(None, chan, None, None),
            P(),
            P(),
            P(),
        ),
        out_specs=P(chan, "tm"),
        check_vma=False,
    )
```

time: 411 us -> 290 us (0.71)
  matrix products: 137 us -> 0 us
  Pallas kernels: 0 us -> 98.7 us
  waiting for transfers between devices: 177 us -> 108 us
  starting transfers between devices: 7.45 us -> 46.5 us
  other arithmetic: 35.5 us -> 0.15 us
  loops' own time: 24.5 us -> 0 us
  local copies, waits for them, and re-layouts: 18.3 us -> 26 us
    dot_general x72 -> x0, matrix products: 137 us -> none  [the longest x24 92.1 us: fdot(): return jnp.dot(left, right, preferred_element_type=jnp.float32)]
    all_to_all x1 -> x3, waiting for transfers between devices: 177 us -> 51 us  [body(): lax.all_to_all(picked, ('lo', 'tm'), split_axis=0, concat_axis=0, tiled=T...]
    pallas_call x0 -> x23, Pallas kernels: none -> 98.7 us  [the longest x18 54.5 us: iterate(): pl.pallas_call(functools.partial(iterate_kernel, first), out_shape=jax.Sh...]
    ppermute x0 -> x20, waiting for transfers between devices: none -> 57.4 us  [the longest x1 56.3 us: body(): far_windows = lax.ppermute(own_windows, 'hi', SWAP)]
    ppermute x0 -> x20, starting transfers between devices: none -> 29.9 us  [the longest x18 26.9 us: body(): images = (image, lax.ppermute(image, 'hi', SWAP))]
    reduce_sum x112 -> x0, other arithmetic: 26.5 us -> none  [the longest x56 16.2 us: orthonormal(): jnp.sum(prev_real * vec_real + prev_imag * vec_imag, axis=-1, keepdims=True)]
    another operation x1 -> x0, loops' own time: 24.5 us -> none  [body(): lax.map(one_channel, (volt_real, volt_imag, base_real, base_imag, channel...]
    unnamed x23 -> x29, local copies, waits for them, and re-layouts: 0.33 us -> 11.3 us
  transfers between devices with their start and end apart: 1 -> 23, of which waited for: 1 -> 4; matrix products, arithmetic and copies ran while one was open for 2% -> 5% of each run, Pallas kernels for 0% -> 28%
where the time goes in v1:
time: 290 us
  waiting for transfers between devices  108 us (37%)
  Pallas kernels  98.7 us (34%)
  starting transfers between devices  46.5 us (16%)
  local copies, waits for them, and re-layouts  26 us (9%)
  blocking collectives  9.59 us (3%)
    ppermute x1, waiting for transfers between devices, body(): far_windows = lax.ppermute(own_windows, 'hi', SWAP)  56.3 us
    pallas_call x18, Pallas kernels, iterate(): pl.pallas_call(functools.partial(iterate_kernel, first), out_shape=jax.Sh...  54.5 us
    all_to_all x3, waiting for transfers between devices, body(): lax.all_to_all(picked, ('lo', 'tm'), split_axis=0, concat_axis=0, tiled=T...  51 us
    pallas_call x4, Pallas kernels, beam_power(): pl.pallas_call(functools.partial(beam_kernel, at), out_shape=jax.ShapeDty...  31.2 us
    ppermute x18, starting transfers between devices, body(): images = (image, lax.ppermute(image, 'hi', SWAP))  26.9 us
    all_to_all x3, starting transfers between devices, body(): lax.all_to_all(picked, ('lo', 'tm'), split_axis=0, concat_axis=0, tiled=T...  16.6 us
    pallas_call x1, Pallas kernels, steering(): pl.pallas_call(steer_kernel, out_shape=jax.ShapeDtypeStruct((channels, 2,...  12.9 us
    unnamed x29, local copies, waits for them, and re-layouts  11.3 us
  transfers between devices with their start and end apart: 23, of which 4 were waited for; matrix products, arithmetic and copies ran while one was open for 5% of the time, Pallas kernels for 28%

profile of v1, /device:TPU:0, one launch (start us, length us, event | category | flops | bytes accessed | tf_op | source)
XLA Modules:
  0.0 289.7 jit_solution(2720158595336065269)
XLA Ops:
  0.0 4.0 %fusion.3 = (bf16[2,1,16,1,64,512]{5,4,3,2,1,0:T(8,128)(2,1)S(1)}, bf16[2,1,16,1,64,512]{5,4,3,2,1,0:T(8,128)(2,1)}) fusion(bf16[2,2,16,2,64,512]{5,4,3,2,1,0:T(8,128)(2,1)} %bitcast.46), kind=kLoop, calls=%fused_computation.20 | loop fusion | bytes 8388608 | tf_op jit(solution)/shard_map/slice | solution.py:220
  5.5 6.3 %all-to-all-start.1 = ((bf16[16,2,1,64,512]{4,3,2,1,0:T(8,128)(2,1)}), bf16[16,2,1,64,512]{4,3,2,1,0:T(8,128)(2,1)S(1)}, u32[]{:S(2)}, u32[]{:S(2)}) async-start(bf16[16,2,1,64,512]{4,3,2,1,0:T(8,128)(2,1)} %bitcast.49), calls=%async_computation.1 | async-start | bytes 4194304 | tf_op jit(solution)/shard_map/all_to_all | solution.py:222
  11.8 3.2 %copy.56 = bf16[2,1,16,1,64,512]{5,4,0,2,3,1:T(8,128)(2,1)} copy(bf16[2,1,16,1,64,512]{5,4,3,2,1,0:T(8,128)(2,1)} %get-tuple-element.6) | data formatting | bytes 4194304
  15.0 25.8 %all-to-all-done.1.refs_1_.refs_2_.volt_ref = bf16[16,2,1,64,512]{4,3,2,1,0:T(8,128)(2,1)S(1)} async-done(((bf16[16,2,1,64,512]{4,3,2,1,0:T(8,128)(2,1)}), bf16[16,2,1,64,512]{4,3,2,1,0:T(8,128)(2,1)S(1)}, u32[]{:S(2)}, u32[]{:S(2)}) %all-to-all-start.1) | async-done | bytes 2097184 | tf_op jit(solution)/shard_map/all_to_all | solution.py:222
  42.2 5.2 %all-to-all-start.2 = ((bf16[16,2,1,64,512]{4,3,2,1,0:T(8,128)(2,1)}), bf16[16,2,1,64,512]{4,3,2,1,0:T(8,128)(2,1)S(1)}, u32[]{:S(2)}, u32[]{:S(2)}) async-start(bf16[16,2,1,64,512]{4,3,2,1,0:T(8,128)(2,1)} %bitcast.48), calls=%async_computation.2 | async-start | bytes 4194304 | tf_op jit(solution)/shard_map/all_to_all | solution.py:222
  47.3 4.7 %copy_bitcast_fusion = bf16[16,2,2,64,512]{4,3,2,1,0:T(8,128)(2,1)} fusion(bf16[2,2,16,2,64,512]{5,4,3,2,1,0:T(8,128)(2,1)} %bitcast.47), kind=kLoop, calls=%fused_computation.1 | loop fusion | bytes 8388608 | tf_op jit(solution)/shard_map/transpose | solution.py:221
  52.1 25.2 %all-to-all-done.2.refs_1_.refs_2_.volt_ref = bf16[16,2,1,64,512]{4,3,2,1,0:T(8,128)(2,1)S(1)} async-done(((bf16[16,2,1,64,512]{4,3,2,1,0:T(8,128)(2,1)}), bf16[16,2,1,64,512]{4,3,2,1,0:T(8,128)(2,1)S(1)}, u32[]{:S(2)}, u32[]{:S(2)}) %all-to-all-start.2) | async-done | bytes 2097184 | tf_op jit(solution)/shard_map/all_to_all | solution.py:222
  77.3 5.1 %all-to-all-start = ((bf16[16,2,2,64,512]{4,3,2,1,0:T(8,128)(2,1)}), bf16[16,2,2,64,512]{4,3,2,1,0:T(8,128)(2,1)}, u32[]{:S(2)}, u32[]{:S(2)}) async-start(bf16[16,2,2,64,512]{4,3,2,1,0:T(8,128)(2,1)} %copy_bitcast_fusion), calls=%async_computation | async-start | bytes 8388608 | tf_op jit(solution)/shard_map/all_to_all | solution.py:222
  85.6 56.3 %collective-permute-done = s32[2,2]{1,0:T(2,128)S(1)} collective-permute-done((s32[2,2]{1,0:T(2,128)S(1)}, s32[2,2]{1,0:T(2,128)S(1)}, u32[]{:S(2)}, u32[]{:S(2)}) %collective-permute-start) | collective-permute-done | bytes 48 | tf_op jit(solution)/shard_map/ppermute | solution.py:227
  146.8 3.4 %collective-permute-start.8 = (f32[1,16,512]{2,1,0:T(8,128)S(1)}, f32[1,16,512]{2,1,0:T(8,128)S(1)}, u32[]{:S(2)}, u32[]{:S(2)}) collective-permute-start(f32[1,16,512]{2,1,0:T(8,128)S(1)} %iterate.24.refs_0_), channel_id=1, source_target_pairs={{0,16},{16,0},{1,17},{17,1},{2,18},{18,2},{3,19},{19,3},{4,20},{20... | collective-permute-start | bytes 98312 | tf_op jit(solution)/shard_map/ppermute | solution.py:255
  154.6 2.9 %collective-permute-start.9 = (f32[1,16,512]{2,1,0:T(8,128)S(1)}, f32[1,16,512]{2,1,0:T(8,128)S(1)}, u32[]{:S(2)}, u32[]{:S(2)}) collective-permute-start(f32[1,16,512]{2,1,0:T(8,128)S(1)} %iterate.25.refs_0_), channel_id=1, source_target_pairs={{0,16},{16,0},{1,17},{17,1},{2,18},{18,2},{3,19},{19,3},{4,20},{20... | collective-permute-start | bytes 98312 | tf_op jit(solution)/shard_map/ppermute | solution.py:255
  164.9 4.8 %iterate.18.refs_0_ = f32[2,16,512]{2,1,0:T(8,128)S(1)} custom-call(s32[2,2]{1,0:T(2,128)S(1)} %get-tuple-element.11.win_ref, s32[1]{0:T(128)} %bitcast.start_ref, f32[2,16,512]{2,1,0:T(8,128)S(1)} %get-tuple-element.7.refs_0_, bf16[16,2,2,64,512]{4,3,2,1,0:T(8,128)(2,1)} %all-to-all-done.refs_1_.refs_2_.volt_ref), custom_call_target="tpu_custom_call" | custom-call | flops 134217728 | bytes 4194304 | tf_op jit(solution)/shard_map/iterate/pallas_call | solution.py:87
  177.1 4.7 %iterate.19.refs_0_ = f32[2,16,512]{2,1,0:T(8,128)S(1)} custom-call(s32[2,2]{1,0:T(2,128)S(1)} %get-tuple-element.11.win_ref, s32[1]{0:T(128)} %bitcast.start_ref, f32[2,16,512]{2,1,0:T(8,128)S(1)} %iterate.18.refs_0_, f32[2,16,512]{2,1,0:T(8,128)S(1)} %collective-permute-done.2.refs_1_, bf16[16,2,2,64,512]{4,3,2,1,0:T(8,128)(2,1)} %all-to-all-done.refs_1_.refs_2_.volt_ref), custom_call_target="tpu_custom_call" | custom-call | flops 134217728 | bytes 4194304 | tf_op jit(solution)/shard_map/iterate/pallas_call | solution.py:87
  184.9 4.0 %gather_fusion = f32[1024,2]{1,0:T(8,128)} fusion(f32[2,1024]{0,1:T(8,128)S(1)} %copy.39, s32[1024]{0:T(1024)S(1)} %fusion), kind=kCustom, calls=%fused_computation | custom fusion | bytes 20480 | tf_op jit(solution)/shard_map/jit(_take)/gather | solution.py:237
  199.1 4.7 %iterate.20.refs_0_ = f32[2,16,512]{2,1,0:T(8,128)S(1)} custom-call(s32[2,2]{1,0:T(2,128)S(1)} %get-tuple-element.11.win_ref, s32[1]{0:T(128)} %bitcast.start_ref, f32[2,16,512]{2,1,0:T(8,128)S(1)} %iterate.19.refs_0_, f32[2,16,512]{2,1,0:T(8,128)S(1)} %collective-permute-done.3.refs_1_, bf16[16,2,2,64,512]{4,3,2,1,0:T(8,128)(2,1)} %all-to-all-done.refs_1_.refs_2_.volt_ref), custom_call_target="tpu_custom_call" | custom-call | flops 134217728 | bytes 4194304 | tf_op jit(solution)/shard_map/iterate/pallas_call | solution.py:87
  212.8 4.7 %iterate.21.refs_0_ = f32[2,16,512]{2,1,0:T(8,128)S(1)} custom-call(s32[2,2]{1,0:T(2,128)S(1)} %get-tuple-element.11.win_ref, s32[1]{0:T(128)} %bitcast.start_ref, f32[2,16,512]{2,1,0:T(8,128)S(1)} %iterate.20.refs_0_, f32[2,16,512]{2,1,0:T(8,128)S(1)} %collective-permute-done.4.refs_1_, bf16[16,2,2,64,512]{4,3,2,1,0:T(8,128)(2,1)} %all-to-all-done.refs_1_.refs_2_.volt_ref), custom_call_target="tpu_custom_call" | custom-call | flops 134217728 | bytes 4194304 | tf_op jit(solution)/shard_map/iterate/pallas_call | solution.py:87
  220.6 12.9 %steering.1.steer_ref = bf16[4,2,512,1024]{3,2,1,0:T(8,128)(2,1)S(1)} custom-call(f32[4]{0:T(128)S(1)} %fusion.2.freq_ref, f32[512,2]{1,0:T(8,128)S(1)} %bitcast.41, f32[2,1024]{1,0:T(2,128)S(1)} %select_bitcast_fusion.toward_ref), custom_call_target="tpu_custom_call" | custom-call | flops 83886080 | bytes 8388608 | tf_op jit(solution)/shard_map/steering/pallas_call | solution.py:182
  235.8 4.7 %iterate.22.refs_0_ = f32[2,16,512]{2,1,0:T(8,128)S(1)} custom-call(s32[2,2]{1,0:T(2,128)S(1)} %get-tuple-element.11.win_ref, s32[1]{0:T(128)} %bitcast.start_ref, f32[2,16,512]{2,1,0:T(8,128)S(1)} %iterate.21.refs_0_, f32[2,16,512]{2,1,0:T(8,128)S(1)} %collective-permute-done.5.refs_1_, bf16[16,2,2,64,512]{4,3,2,1,0:T(8,128)(2,1)} %all-to-all-done.refs_1_.refs_2_.volt_ref), custom_call_target="tpu_custom_call" | custom-call | flops 134217728 | bytes 4194304 | tf_op jit(solution)/shard_map/iterate/pallas_call | solution.py:87
  243.4 7.2 %beams.6 = f32[1,1,1024]{2,1,0:T(1,128)S(1)} custom-call(f32[1,16,512]{2,1,0:T(8,128)S(1)} %iterate.29.own_ref, f32[1,16,512]{2,1,0:T(8,128)S(1)} %collective-permute-done.13.other_ref, bf16[16,2,1,64,512]{4,3,2,1,0:T(8,128)(2,1)S(1)} %copy-done.7, bf16[4,2,512,1024]{3,2,1,0:T(8,128)(2,1)S(1)} %steering.1.steer_ref), custom_call_target="tpu_custom_call" | custom-call | flops 4294967296 | bytes 2097152 | tf_op jit(solution)/shard_map/beams/pallas_call | solution.py:127
  250.6 4.7 %iterate.23.own_ref = f32[2,16,512]{2,1,0:T(8,128)S(1)} custom-call(s32[2,2]{1,0:T(2,128)S(1)} %get-tuple-element.11.win_ref, s32[1]{0:T(128)} %bitcast.start_ref, f32[2,16,512]{2,1,0:T(8,128)S(1)} %iterate.22.refs_0_, f32[2,16,512]{2,1,0:T(8,128)S(1)} %collective-permute-done.6.refs_1_, bf16[16,2,2,64,512]{4,3,2,1,0:T(8,128)(2,1)} %all-to-all-done.refs_1_.refs_2_.volt_ref), custom_call_target="tpu_custom_call" | custom-call | flops 134217728 | bytes 4194304 | tf_op jit(solution)/shard_map/iterate/pallas_call | solution.py:87
  255.3 7.0 %beams.7 = f32[1,1,1024]{2,1,0:T(1,128)S(1)} custom-call(f32[1,16,512]{2,1,0:T(8,128)S(1)} %iterate.35.own_ref, f32[1,16,512]{2,1,0:T(8,128)S(1)} %collective-permute-done.19.other_ref, bf16[16,2,1,64,512]{4,3,2,1,0:T(8,128)(2,1)S(1)} %all-to-all-done.2.refs_1_.refs_2_.volt_ref, bf16[4,2,512,1024]{3,2,1,0:T(8,128)(2,1)S(1)} %steering.1.steer_ref), custom_call_target="tpu_custom_call" | custom-call | flops 4294967296 | bytes 2097152 | tf_op jit(solution)/shard_map/beams/pallas_call | solution.py:127
  262.3 8.5 %beams.4 = f32[1,1,1024]{2,1,0:T(1,128)S(1)} custom-call(f32[2,16,512]{2,1,0:T(8,128)S(1)} %iterate.23.own_ref, f32[2,16,512]{2,1,0:T(8,128)S(1)} %collective-permute-done.7.other_ref, bf16[16,2,2,64,512]{4,3,2,1,0:T(8,128)(2,1)} %all-to-all-done.refs_1_.refs_2_.volt_ref, bf16[4,2,512,1024]{3,2,1,0:T(8,128)(2,1)S(1)} %steering.1.steer_ref), custom_call_target="tpu_custom_call" | custom-call | flops 4294967296 | bytes 2097152 | tf_op jit(solution)/shard_map/beams/pallas_call | solution.py:127
  270.9 8.5 %beams.5 = f32[1,1,1024]{2,1,0:T(1,128)S(1)} custom-call(f32[2,16,512]{2,1,0:T(8,128)S(1)} %iterate.23.own_ref, f32[2,16,512]{2,1,0:T(8,128)S(1)} %collective-permute-done.7.other_ref, bf16[16,2,2,64,512]{4,3,2,1,0:T(8,128)(2,1)} %all-to-all-done.refs_1_.refs_2_.volt_ref, bf16[4,2,512,1024]{3,2,1,0:T(8,128)(2,1)S(1)} %steering.1.steer_ref), custom_call_target="tpu_custom_call" | custom-call | flops 4294967296 | bytes 2097152 | tf_op jit(solution)/shard_map/beams/pallas_call | solution.py:127
  279.5 9.6 %all_to_all.20 = f32[4,2,512]{2,1,0:T(2,128)S(1)} all-to-all(f32[4,2,512]{2,1,0:T(2,128)S(1)} %bitcast.51), channel_id=1, replica_groups=mesh['hi'=2,'lo'=8,'tm'=2] {'hi','tm'}, dimensions={0} | all-to-all | bytes 32768 | tf_op jit(solution)/shard_map/all_to_all | solution.py:261
  (94 shorter events, 61.3 us)
Async XLA Ops:
  0.0 85.2 %copy-start = (f32[2,4,8,512]{3,2,1,0:T(8,128)S(1)}, f32[2,4,8,512]{3,2,1,0:T(8,128)}, u32[]{:S(2)}) copy-start(f32[2,4,8,512]{3,2,1,0:T(8,128)} %param.8) | copy-start | bytes 393220
  5.5 35.3 %all-to-all-start.1 = ((bf16[16,2,1,64,512]{4,3,2,1,0:T(8,128)(2,1)}), bf16[16,2,1,64,512]{4,3,2,1,0:T(8,128)(2,1)S(1)}, u32[]{:S(2)}, u32[]{:S(2)}) async-start(bf16[16,2,1,64,512]{4,3,2,1,0:T(8,128)(2,1)} %bitcast.49), calls=%async_computation.1 | async-start | bytes 4194304 | tf_op jit(solution)/shard_map/all_to_all | solution.py:222
  42.2 35.1 %all-to-all-start.2 = ((bf16[16,2,1,64,512]{4,3,2,1,0:T(8,128)(2,1)}), bf16[16,2,1,64,512]{4,3,2,1,0:T(8,128)(2,1)S(1)}, u32[]{:S(2)}, u32[]{:S(2)}) async-start(bf16[16,2,1,64,512]{4,3,2,1,0:T(8,128)(2,1)} %bitcast.48), calls=%async_computation.2 | async-start | bytes 4194304 | tf_op jit(solution)/shard_map/all_to_all | solution.py:222
  77.3 87.6 %all-to-all-start = ((bf16[16,2,2,64,512]{4,3,2,1,0:T(8,128)(2,1)}), bf16[16,2,2,64,512]{4,3,2,1,0:T(8,128)(2,1)}, u32[]{:S(2)}, u32[]{:S(2)}) async-start(bf16[16,2,2,64,512]{4,3,2,1,0:T(8,128)(2,1)} %copy_bitcast_fusion), calls=%async_computation | async-start | bytes 8388608 | tf_op jit(solution)/shard_map/all_to_all | solution.py:222
  82.6 59.3 %collective-permute-start = (s32[2,2]{1,0:T(2,128)S(1)}, s32[2,2]{1,0:T(2,128)S(1)}, u32[]{:S(2)}, u32[]{:S(2)}) collective-permute-start(s32[2,2]{1,0:T(2,128)S(1)} %copy.44), channel_id=1, source_target_pairs={{0,16},{16,0},{1,17},{17,1},{2,18},{18,2},{3,19},{19,3},{4,20},{20... | collective-permute-start | bytes 56 | tf_op jit(solution)/shard_map/ppermute | solution.py:227
  85.2 57.8 %collective-permute-start.1 = (f32[2,16,512]{2,1,0:T(8,128)S(1)}, f32[2,16,512]{2,1,0:T(8,128)S(1)}, u32[]{:S(2)}, u32[]{:S(2)}) collective-permute-start(f32[2,16,512]{2,1,0:T(8,128)S(1)} %copy_bitcast_fusion.3), channel_id=1, source_target_pairs={{0,16},{16,0},{1,17},{17,1},{2,18},{18,2},{3,19},{19,3},{4,20},{20... | collective-permute-start | bytes 196616 | tf_op jit(solution)/shard_map/ppermute | solution.py:228
  146.8 5.6 %collective-permute-start.8 = (f32[1,16,512]{2,1,0:T(8,128)S(1)}, f32[1,16,512]{2,1,0:T(8,128)S(1)}, u32[]{:S(2)}, u32[]{:S(2)}) collective-permute-start(f32[1,16,512]{2,1,0:T(8,128)S(1)} %iterate.24.refs_0_), channel_id=1, source_target_pairs={{0,16},{16,0},{1,17},{17,1},{2,18},{18,2},{3,19},{19,3},{4,20},{20... | collective-permute-start | bytes 98312 | tf_op jit(solution)/shard_map/ppermute | solution.py:255
  152.4 5.1 %collective-permute-start.14 = (f32[1,16,512]{2,1,0:T(8,128)S(1)}, f32[1,16,512]{2,1,0:T(8,128)S(1)}, u32[]{:S(2)}, u32[]{:S(2)}) collective-permute-start(f32[1,16,512]{2,1,0:T(8,128)S(1)} %iterate.30.refs_0_), channel_id=1, source_target_pairs={{0,16},{16,0},{1,17},{17,1},{2,18},{18,2},{3,19},{19,3},{4,20},{20... | collective-permute-start | bytes 98312 | tf_op jit(solution)/shard_map/ppermute | solution.py:255
  154.6 5.1 %collective-permute-start.9 = (f32[1,16,512]{2,1,0:T(8,128)S(1)}, f32[1,16,512]{2,1,0:T(8,128)S(1)}, u32[]{:S(2)}, u32[]{:S(2)}) collective-permute-start(f32[1,16,512]{2,1,0:T(8,128)S(1)} %iterate.25.refs_0_), channel_id=1, source_target_pairs={{0,16},{16,0},{1,17},{17,1},{2,18},{18,2},{3,19},{19,3},{4,20},{20... | collective-permute-start | bytes 98312 | tf_op jit(solution)/shard_map/ppermute | solution.py:255
  159.7 10.0 %collective-permute-start.15 = (f32[1,16,512]{2,1,0:T(8,128)S(1)}, f32[1,16,512]{2,1,0:T(8,128)S(1)}, u32[]{:S(2)}, u32[]{:S(2)}) collective-permute-start(f32[1,16,512]{2,1,0:T(8,128)S(1)} %iterate.31.refs_0_), channel_id=1, source_target_pairs={{0,16},{16,0},{1,17},{17,1},{2,18},{18,2},{3,19},{19,3},{4,20},{20... | collective-permute-start | bytes 98312 | tf_op jit(solution)/shard_map/ppermute | solution.py:255
  161.9 12.9 %collective-permute-start.10 = (f32[1,16,512]{2,1,0:T(8,128)S(1)}, f32[1,16,512]{2,1,0:T(8,128)S(1)}, u32[]{:S(2)}, u32[]{:S(2)}) collective-permute-start(f32[1,16,512]{2,1,0:T(8,128)S(1)} %iterate.26.refs_0_), channel_id=1, source_target_pairs={{0,16},{16,0},{1,17},{17,1},{2,18},{18,2},{3,19},{19,3},{4,20},{20... | collective-permute-start | bytes 98312 | tf_op jit(solution)/shard_map/ppermute | solution.py:255
  169.7 7.4 %collective-permute-start.2 = (f32[2,16,512]{2,1,0:T(8,128)S(1)}, f32[2,16,512]{2,1,0:T(8,128)S(1)}, u32[]{:S(2)}, u32[]{:S(2)}) collective-permute-start(f32[2,16,512]{2,1,0:T(8,128)S(1)} %iterate.18.refs_0_), channel_id=1, source_target_pairs={{0,16},{16,0},{1,17},{17,1},{2,18},{18,2},{3,19},{19,3},{4,20},{20... | collective-permute-start | bytes 196616 | tf_op jit(solution)/shard_map/ppermute | solution.py:255
  171.9 18.2 %collective-permute-start.16 = (f32[1,16,512]{2,1,0:T(8,128)S(1)}, f32[1,16,512]{2,1,0:T(8,128)S(1)}, u32[]{:S(2)}, u32[]{:S(2)}) collective-permute-start(f32[1,16,512]{2,1,0:T(8,128)S(1)} %iterate.32.refs_0_), channel_id=1, source_target_pairs={{0,16},{16,0},{1,17},{17,1},{2,18},{18,2},{3,19},{19,3},{4,20},{20... | collective-permute-start | bytes 98312 | tf_op jit(solution)/shard_map/ppermute | solution.py:255
  177.1 15.4 %collective-permute-start.11 = (f32[1,16,512]{2,1,0:T(8,128)S(1)}, f32[1,16,512]{2,1,0:T(8,128)S(1)}, u32[]{:S(2)}, u32[]{:S(2)}) collective-permute-start(f32[1,16,512]{2,1,0:T(8,128)S(1)} %iterate.27.refs_0_), channel_id=1, source_target_pairs={{0,16},{16,0},{1,17},{17,1},{2,18},{18,2},{3,19},{19,3},{4,20},{20... | collective-permute-start | bytes 98312 | tf_op jit(solution)/shard_map/ppermute | solution.py:255
  181.8 17.3 %collective-permute-start.3 = (f32[2,16,512]{2,1,0:T(8,128)S(1)}, f32[2,16,512]{2,1,0:T(8,128)S(1)}, u32[]{:S(2)}, u32[]{:S(2)}) collective-permute-start(f32[2,16,512]{2,1,0:T(8,128)S(1)} %iterate.19.refs_0_), channel_id=1, source_target_pairs={{0,16},{16,0},{1,17},{17,1},{2,18},{18,2},{3,19},{19,3},{4,20},{20... | collective-permute-start | bytes 196616 | tf_op jit(solution)/shard_map/ppermute | solution.py:255
  192.4 11.5 %collective-permute-start.17 = (f32[1,16,512]{2,1,0:T(8,128)S(1)}, f32[1,16,512]{2,1,0:T(8,128)S(1)}, u32[]{:S(2)}, u32[]{:S(2)}) collective-permute-start(f32[1,16,512]{2,1,0:T(8,128)S(1)} %iterate.33.refs_0_), channel_id=1, source_target_pairs={{0,16},{16,0},{1,17},{17,1},{2,18},{18,2},{3,19},{19,3},{4,20},{20... | collective-permute-start | bytes 98312 | tf_op jit(solution)/shard_map/ppermute | solution.py:255
  196.2 12.8 %collective-permute-start.12 = (f32[1,16,512]{2,1,0:T(8,128)S(1)}, f32[1,16,512]{2,1,0:T(8,128)S(1)}, u32[]{:S(2)}, u32[]{:S(2)}) collective-permute-start(f32[1,16,512]{2,1,0:T(8,128)S(1)} %iterate.28.refs_0_), channel_id=1, source_target_pairs={{0,16},{16,0},{1,17},{17,1},{2,18},{18,2},{3,19},{19,3},{4,20},{20... | collective-permute-start | bytes 98312 | tf_op jit(solution)/shard_map/ppermute | solution.py:255
  203.8 9.0 %collective-permute-start.4 = (f32[2,16,512]{2,1,0:T(8,128)S(1)}, f32[2,16,512]{2,1,0:T(8,128)S(1)}, u32[]{:S(2)}, u32[]{:S(2)}) collective-permute-start(f32[2,16,512]{2,1,0:T(8,128)S(1)} %iterate.20.refs_0_), channel_id=1, source_target_pairs={{0,16},{16,0},{1,17},{17,1},{2,18},{18,2},{3,19},{19,3},{4,20},{20... | collective-permute-start | bytes 196616 | tf_op jit(solution)/shard_map/ppermute | solution.py:255
  206.0 27.5 %collective-permute-start.18 = (f32[1,16,512]{2,1,0:T(8,128)S(1)}, f32[1,16,512]{2,1,0:T(8,128)S(1)}, u32[]{:S(2)}, u32[]{:S(2)}) collective-permute-start(f32[1,16,512]{2,1,0:T(8,128)S(1)} %iterate.34.refs_0_), channel_id=1, source_target_pairs={{0,16},{16,0},{1,17},{17,1},{2,18},{18,2},{3,19},{19,3},{4,20},{20... | collective-permute-start | bytes 98312 | tf_op jit(solution)/shard_map/ppermute | solution.py:255
  212.7 30.7 %collective-permute-start.13 = (f32[1,16,512]{2,1,0:T(8,128)S(1)}, f32[1,16,512]{2,1,0:T(8,128)S(1)}, u32[]{:S(2)}, u32[]{:S(2)}) collective-permute-start(f32[1,16,512]{2,1,0:T(8,128)S(1)} %iterate.29.own_ref), channel_id=1, source_target_pairs={{0,16},{16,0},{1,17},{17,1},{2,18},{18,2},{3,19},{19,3},{4,20},{20... | collective-permute-start | bytes 98312 | tf_op jit(solution)/shard_map/ppermute | solution.py:255
  217.5 18.3 %collective-permute-start.5 = (f32[2,16,512]{2,1,0:T(8,128)S(1)}, f32[2,16,512]{2,1,0:T(8,128)S(1)}, u32[]{:S(2)}, u32[]{:S(2)}) collective-permute-start(f32[2,16,512]{2,1,0:T(8,128)S(1)} %iterate.21.refs_0_), channel_id=1, source_target_pairs={{0,16},{16,0},{1,17},{17,1},{2,18},{18,2},{3,19},{19,3},{4,20},{20... | collective-permute-start | bytes 196616 | tf_op jit(solution)/shard_map/ppermute | solution.py:255
  235.8 19.6 %collective-permute-start.19 = (f32[1,16,512]{2,1,0:T(8,128)S(1)}, f32[1,16,512]{2,1,0:T(8,128)S(1)}, u32[]{:S(2)}, u32[]{:S(2)}) collective-permute-start(f32[1,16,512]{2,1,0:T(8,128)S(1)} %iterate.35.own_ref), channel_id=1, source_target_pairs={{0,16},{16,0},{1,17},{17,1},{2,18},{18,2},{3,19},{19,3},{4,20},{20... | collective-permute-start | bytes 98312 | tf_op jit(solution)/shard_map/ppermute | solution.py:255
  240.5 10.1 %collective-permute-start.6 = (f32[2,16,512]{2,1,0:T(8,128)S(1)}, f32[2,16,512]{2,1,0:T(8,128)S(1)}, u32[]{:S(2)}, u32[]{:S(2)}) collective-permute-start(f32[2,16,512]{2,1,0:T(8,128)S(1)} %iterate.22.refs_0_), channel_id=1, source_target_pairs={{0,16},{16,0},{1,17},{17,1},{2,18},{18,2},{3,19},{19,3},{4,20},{20... | collective-permute-start | bytes 196616 | tf_op jit(solution)/shard_map/ppermute | solution.py:255
  255.3 7.0 %collective-permute-start.7 = (f32[2,16,512]{2,1,0:T(8,128)S(1)}, f32[2,16,512]{2,1,0:T(8,128)S(1)}, u32[]{:S(2)}, u32[]{:S(2)}) collective-permute-start(f32[2,16,512]{2,1,0:T(8,128)S(1)} %iterate.23.own_ref), channel_id=1, source_target_pairs={{0,16},{16,0},{1,17},{17,1},{2,18},{18,2},{3,19},{19,3},{4,20},{20... | collective-permute-start | bytes 196616 | tf_op jit(solution)/shard_map/ppermute | solution.py:255
  (11 other events, 110.8 us)

commit v2 on v1

v2 whole, which is shorter than its diff:
```python
import functools

import jax
import jax.numpy as jnp
import numpy as np
from jax import lax
from jax.experimental import pallas as pl
from jax.experimental.pallas import tpu as pltpu
from jax.sharding import Mesh
from jax.sharding import PartitionSpec as P

ITERS = 6
EPS = 1e-06
F32 = jnp.float32
BF16 = jnp.bfloat16
VMEM = pl.BlockSpec(memory_space=pltpu.VMEM)
SMEM = pl.BlockSpec(memory_space=pltpu.SMEM)
ANY = pl.BlockSpec(memory_space=pl.ANY)
VMEM_LIMIT = 40 << 20


def orthonormal(chans):
    number = chans[0][0].shape[0]
    row = lax.broadcasted_iota(jnp.int32, (number, 1), 0)
    for j in range(number):
        after = []
        for re, im in chans:
            top_re, top_im = re[j : j + 1], im[j : j + 1]
            dot_re = jnp.sum(top_re * re + top_im * im, axis=1, keepdims=True)
            dot_im = jnp.sum(top_re * im - top_im * re, axis=1, keepdims=True)
            inverse = lax.rsqrt(dot_re[j : j + 1] + EPS)
            share = jnp.where(row > j, inverse * inverse, 0.0)
            coef_re, coef_im = share * dot_re, share * dot_im
            scale = jnp.where(row == j, inverse, 1.0)
            after.append(
                (
                    re * scale - (coef_re * top_re - coef_im * top_im),
                    im * scale - (coef_re * top_im + coef_im * top_re),
                )
            )
        chans = after
    return chans


def contract(left, right, at_left, at_right):
    return lax.dot_general(
        left, right, (((at_left,), (at_right,)), ((), ())), preferred_element_type=F32
    )


def project(base_re, base_im, volt_re, volt_im):
    first = jnp.concatenate([base_re, -base_im], 0).astype(BF16)
    second = jnp.concatenate([base_im, base_re], 0).astype(BF16)
    return contract(first, volt_re, 1, 1) + contract(second, volt_im, 1, 1)


def split(stacked):
    number = stacked.shape[0] // 2
    return stacked[:number], stacked[number:]


def images_of(image_refs, at):
    total = image_refs[0][at].astype(F32)
    for ref in image_refs[1:]:
        total = total + ref[at].astype(F32)
    return split(total)


def channels_of(volt_refs):
    for ref in volt_refs:
        sources, _, members, rows, stations = ref.shape
        for m in range(members):
            yield tuple(ref[:, part, m].reshape(sources * rows, stations) for part in range(2))


def iterate_kernel(n_images, n_volt, win_ref, start_ref, *refs):
    image_refs, volt_refs, out_ref = refs[:n_images], refs[n_images : n_images + n_volt], refs[-1]
    channels, number = out_ref.shape[0], out_ref.shape[1] // 2
    total = volt_refs[0].shape[0] * volt_refs[0].shape[3]
    bases = orthonormal([images_of(image_refs, c) for c in range(channels)])
    sample = start_ref[0] + lax.broadcasted_iota(jnp.int32, (1, total), 1)
    for c, (volt_re, volt_im) in enumerate(channels_of(volt_refs)):
        proj = project(*bases[c], volt_re, volt_im)
        inside = (sample >= win_ref[c, 0]) & (sample < win_ref[c, 1])
        proj = jnp.where(inside, proj, 0.0).astype(BF16)
        by_re = contract(proj, volt_re, 1, 0)
        by_im = contract(proj, volt_im, 1, 0)
        out_ref[c, :number] = (by_re[:number] - by_im[number:]).astype(out_ref.dtype)
        out_ref[c, number:] = (by_im[:number] + by_re[number:]).astype(out_ref.dtype)


def iterate(windows, start, images, volts, after):
    moved = sum(v.size for v in volts)
    return pl.pallas_call(
        functools.partial(iterate_kernel, len(images), len(volts)),
        out_shape=jax.ShapeDtypeStruct(images[0].shape, BF16),
        in_specs=[SMEM, SMEM] + [VMEM] * (len(images) + len(volts)) + [ANY] * len(after),
        out_specs=VMEM,
        compiler_params=pltpu.CompilerParams(vmem_limit_bytes=VMEM_LIMIT),
        cost_estimate=pl.CostEstimate(
            flops=moved * 64, bytes_accessed=moved * 2, transcendentals=0
        ),
        name="iterate",
    )(windows, start, *images, *volts, *after)


def raw_kernel(volt_ref, steer_ref, *refs):
    out_ref = refs[-1]
    ((volt_re, volt_im),) = channels_of([volt_ref])
    steer_re, steer_im = steer_ref[0, 0], steer_ref[0, 1]
    beam_re = contract(volt_re, steer_re, 1, 0) + contract(volt_im, steer_im, 1, 0)
    beam_im = contract(volt_im, steer_re, 1, 0) - contract(volt_re, steer_im, 1, 0)
    out_ref[0] = jnp.sum(beam_re * beam_re + beam_im * beam_im, axis=0, keepdims=True)


def raw_power(volt, at, steer, channel, first, width, tile, after):
    sources, parts, _, rows, stations = volt.shape
    return pl.pallas_call(
        raw_kernel,
        out_shape=jax.ShapeDtypeStruct((1, 1, width), F32),
        grid=(width // tile,),
        in_specs=[
            pl.BlockSpec((sources, parts, 1, rows, stations), lambda i: (0, 0, at, 0, 0)),
            pl.BlockSpec(
                (1, parts, stations, tile), lambda i: (channel, 0, 0, first // tile + i)
            ),
        ]
        + [ANY] * len(after),
        out_specs=pl.BlockSpec((1, 1, tile), lambda i: (0, 0, i)),
        compiler_params=pltpu.CompilerParams(vmem_limit_bytes=VMEM_LIMIT),
        cost_estimate=pl.CostEstimate(
            flops=sources * rows * stations * width * 8,
            bytes_accessed=stations * width * 4,
            transcendentals=0,
        ),
        name="raw_power",
    )(volt, steer, *after)


def null_kernel(n_volt, own_ref, other_ref, raw_ref, steer_ref, *refs):
    volt_refs, out_ref, base_ref = refs[:n_volt], refs[n_volt], refs[n_volt + 1]
    channels = own_ref.shape[0]

    @pl.when(pl.program_id(0) == 0)
    def _():
        made = orthonormal([images_of((own_ref, other_ref), c) for c in range(channels)])
        for c, (base_re, base_im) in enumerate(made):
            base_ref[c] = jnp.concatenate([base_re, base_im], 0)

    for c, (volt_re, volt_im) in enumerate(channels_of(volt_refs)):

        @pl.when(pl.program_id(0) == c)
        def _(c=c, volt_re=volt_re, volt_im=volt_im):
            base = base_ref[c]
            base_re, base_im = split(base)
            number = base_re.shape[0]
            full = project(base_re, base_im, volt_re, volt_im).astype(BF16)
            by_re, by_im = contract(full, volt_re, 1, 0), contract(full, volt_im, 1, 0)
            met = jnp.concatenate(
                [by_re[:number] + by_im[number:], by_re[number:] - by_im[:number]], 0
            )
            high = met.astype(BF16)
            low = (met - high.astype(F32)).astype(BF16)
            left = jnp.concatenate([base.astype(BF16), high, low], 0)
            on_re = contract(left, steer_ref[0, 0], 1, 0)
            on_im = contract(left, steer_ref[0, 1], 1, 0)
            base_on_re, base_on_im = on_re[: 2 * number], on_im[: 2 * number]
            met_on_re = on_re[2 * number : 4 * number] + on_re[4 * number :]
            met_on_im = on_im[2 * number : 4 * number] + on_im[4 * number :]
            gain_re = base_on_re[:number] + base_on_im[number:]
            gain_im = base_on_re[number:] - base_on_im[:number]
            met_re = met_on_re[:number] - met_on_im[number:]
            met_im = met_on_im[:number] + met_on_re[number:]
            pairs = contract(full, full, 1, 1)
            pair_re = pairs[:number, :number] + pairs[number:, number:]
            pair_im = pairs[:number, number:] - pairs[number:, :number]
            taken_re, taken_im = -2.0 * met_re, 2.0 * met_im
            for k in range(number):
                top_re, top_im = gain_re[k : k + 1], gain_im[k : k + 1]
                at_re, at_im = pair_re[:, k : k + 1], pair_im[:, k : k + 1]
                taken_re = taken_re + (at_re * top_re - at_im * top_im)
                taken_im = taken_im + (at_re * top_im + at_im * top_re)
            change = jnp.sum(gain_re * taken_re + gain_im * taken_im, axis=0, keepdims=True)
            out_ref[0] = raw_ref[0] + change


def nulled_power(images, raw, volts, steer):
    own, other = images
    channels, parts, stations, beams = steer.shape
    moved = sum(v.size for v in volts)
    same = lambda v: pl.BlockSpec(v.shape, lambda i: (0,) * len(v.shape))
    return pl.pallas_call(
        functools.partial(null_kernel, len(volts)),
        out_shape=jax.ShapeDtypeStruct((channels, 1, beams), F32),
        grid=(channels,),
        in_specs=[
            same(own),
            same(other),
            pl.BlockSpec((1, 1, beams), lambda i: (i, 0, 0)),
            pl.BlockSpec((1, parts, stations, beams), lambda i: (i, 0, 0, 0)),
        ]
        + [VMEM] * len(volts),
        out_specs=pl.BlockSpec((1, 1, beams), lambda i: (i, 0, 0)),
        scratch_shapes=[pltpu.VMEM(own.shape, F32)],
        compiler_params=pltpu.CompilerParams(vmem_limit_bytes=VMEM_LIMIT),
        cost_estimate=pl.CostEstimate(
            flops=moved * 64 + steer.size * 96,
            bytes_accessed=moved * 2 + steer.size * 2,
            transcendentals=0,
        ),
        name="nulled_power",
    )(own, other, raw, steer, *volts)


def turn_series():
    nodes = np.cos((np.arange(4000) + 0.5) / 4000 * np.pi) * 0.25 + 0.25
    angle = 2.0 * np.pi * nodes
    fit = np.polynomial.chebyshev.Chebyshev.fit
    made = []
    for values, degree in ((np.cos(angle), 7), (np.sin(angle) / nodes, 6)):
        series = fit(nodes * nodes, values, degree, domain=[0, 0.25])
        made.append(series.convert(kind=np.polynomial.Polynomial).coef)
    return made


COS_SERIES, SIN_SERIES = turn_series()


def horner(at, series):
    total = jnp.float32(series[-1]) * at + jnp.float32(series[-2])
    for coef in series[-3::-1]:
        total = total * at + jnp.float32(coef)
    return total


def steer_kernel(freq_ref, place_ref, toward_ref, out_ref):
    delay = place_ref[:, 0:1] * toward_ref[0:1, :] + place_ref[:, 1:2] * toward_ref[1:2, :]
    for c in range(out_ref.shape[0]):
        turns = delay * freq_ref[c]
        rest = turns - jnp.round(turns)
        square = rest * rest
        out_ref[c, 0] = horner(square, COS_SERIES).astype(BF16)
        out_ref[c, 1] = (rest * horner(square, SIN_SERIES)).astype(BF16)


def steering(freq, places, toward, tile):
    channels, stations, beams = freq.shape[0], places.shape[0], toward.shape[1]
    return pl.pallas_call(
        steer_kernel,
        out_shape=jax.ShapeDtypeStruct((channels, 2, stations, beams), BF16),
        grid=(beams // tile,),
        in_specs=[
            SMEM,
            pl.BlockSpec((stations, 2), lambda i: (0, 0)),
            pl.BlockSpec((2, tile), lambda i: (0, i)),
        ],
        out_specs=pl.BlockSpec((channels, 2, stations, tile), lambda i: (0, 0, 0, i)),
        compiler_params=pltpu.CompilerParams(vmem_limit_bytes=VMEM_LIMIT),
        cost_estimate=pl.CostEstimate(
            flops=channels * stations * beams * 40,
            bytes_accessed=channels * stations * beams * 4,
            transcendentals=0,
        ),
        name="steering",
    )(freq, places, toward)


SWAP = [(0, 1), (1, 0)]


def body(volt, windows, start_basis, positions, pointing, beam_dir):
    parts, channels_all, rows, stations = volt.shape
    number = start_basis.shape[2]
    n_lo, n_time = lax.axis_size("lo"), lax.axis_size("tm")
    half_at, lo_at, time_at = (lax.axis_index(a) for a in ("hi", "lo", "tm"))
    group = n_lo * n_time
    chan_dev = windows.shape[0]
    per = chan_dev // n_time
    half_time = rows * group
    beams = beam_dir.shape[0]

    blocks = volt.reshape(parts, 2, group, per, rows, stations)
    volts = []
    for owner in range(2):
        picked = jnp.transpose(blocks[:, owner], (1, 0, 2, 3, 4))
        volts.append(lax.all_to_all(picked, ("lo", "tm"), split_axis=0, concat_axis=0, tiled=True))

    own_windows = lax.dynamic_slice_in_dim(windows, time_at * per, per, 0)
    own_basis = lax.dynamic_slice_in_dim(start_basis, time_at * per, per, 1)
    own_basis = jnp.transpose(own_basis, (1, 0, 2, 3)).reshape(per, parts * number, stations)
    far_windows = lax.ppermute(own_windows, "hi", SWAP)
    far_basis = lax.ppermute(own_basis, "hi", SWAP)
    lower = half_at == 0

    def by_owner(own, far):
        return jnp.concatenate([jnp.where(lower, own, far), jnp.where(lower, far, own)])

    all_windows = by_owner(own_windows, far_windows)
    images = (by_owner(own_basis, far_basis),)
    first_sample = (half_at * half_time).astype(jnp.int32).reshape(1)

    toward = jnp.take(pointing, beam_dir, axis=1)
    ids = jnp.arange(per, dtype=jnp.int32) + (lo_at * chan_dev + time_at * per)
    channel_ids = jnp.concatenate([ids, ids + n_lo * chan_dev])
    freq = 1.0 + channel_ids.astype(F32) / channels_all
    steer = steering(freq, positions.T, toward, 128)

    wide = beams // 2
    tile = min(512, wide)
    raw = [
        raw_power(volts[0], i, steer, i, first, wide, tile, ())
        for i in range(per)
        for first in (0, wide)
    ]
    waiting = [(i, first) for i in range(per) for first in (0, wide)]
    after = ()
    for step in range(ITERS):
        image = iterate(all_windows, first_sample, images, volts, after)
        images = (image, lax.ppermute(image, "hi", SWAP))
        after = ()
        share = -(-len(waiting) // (ITERS - step))
        for i, first in waiting[:share]:
            made = raw_power(volts[1], i, steer, per + i, first, wide, tile, (image,))
            raw.append(made)
            after += (made,)
        waiting = waiting[share:]
    raw = jnp.concatenate(raw).reshape(2 * per, 1, beams)
    power = nulled_power(images, raw, volts, steer)
    mine = power.reshape(2, per, n_time, beams // n_time)
    mine = jnp.transpose(mine, (0, 2, 1, 3)) / (2 * half_time * stations)
    flat = mine.reshape(2 * n_time, per, beams // n_time)
    came = lax.all_to_all(flat, ("hi", "tm"), split_axis=0, concat_axis=0, tiled=True)
    came = came.reshape(2, n_time * per, beams // n_time)
    return came[0] + came[1]


def solution(mesh):
    n_chan, n_time = mesh.shape["chan"], mesh.shape["tm"]
    halves = Mesh(mesh.devices.reshape(2, n_chan // 2, n_time), ("hi", "lo", "tm"))
    chan = ("hi", "lo")
    return jax.shard_map(
        body,
        mesh=halves,
        in_specs=(
            P(None, None, ("hi", "lo", "tm"), None),
            P(chan, None),
            P(None, chan, None, None),
            P(),
            P(),
            P(),
        ),
        out_specs=P(chan, "tm"),
        check_vma=False,
    )
```

time: 290 us -> 264 us (0.910); the launches traced: 290 us -> 260 us
  starting transfers between devices: 46.5 us -> 22.8 us
  local copies, waits for them, and re-layouts: 26 us -> 35.9 us
  Pallas kernels: 98.7 us -> 89.3 us
  waiting for transfers between devices: 108 us -> 103 us
    ppermute x1, waiting for transfers between devices: 56.3 us -> 37 us  [body(): far_windows = lax.ppermute(own_windows, 'hi', SWAP)]
    ppermute x18 -> x6, starting transfers between devices: 26.9 us -> 7.93 us  [body(): images = (image, lax.ppermute(image, 'hi', SWAP))]
    pallas_call x0 -> x4, local copies, waits for them, and re-layouts: none -> 16.1 us  [raw_power(): pl.pallas_call(raw_kernel, out_shape=jax.ShapeDtypeStruct((1, 1, width),...]
    ppermute x18 -> x6, waiting for transfers between devices: 0.05 us -> 11.5 us  [body(): images = (image, lax.ppermute(image, 'hi', SWAP))]
    pallas_call x22 -> x11, Pallas kernels: 85.7 us -> 76.2 us  [the longest x6 46.4 us: iterate(): pl.pallas_call(functools.partial(iterate_kernel, len(images), len(volts))...]
    all_to_all x3 -> x2, starting transfers between devices: 16.6 us -> 11.9 us  [body(): lax.all_to_all(picked, ('lo', 'tm'), split_axis=0, concat_axis=0, tiled=T...]
    transpose x1 -> x0, local copies, waits for them, and re-layouts: 4.73 us -> none  [body(): picked = jnp.transpose(picked, (1, 0, 2, 3, 4))]
    all_to_all x3 -> x2, waiting for transfers between devices: 51 us -> 53.9 us  [body(): lax.all_to_all(picked, ('lo', 'tm'), split_axis=0, concat_axis=0, tiled=T...]
  transfers between devices with their start and end apart: 23 -> 10, of which waited for: 4 -> 7; matrix products, arithmetic and copies ran while one was open for 5% -> 9% of each run, Pallas kernels for 28% -> 11%
where the time goes in v2:
time: 264 us; the launch traced here: 260 us
  waiting for transfers between devices  103 us (39%)
  Pallas kernels  89.3 us (34%)
  local copies, waits for them, and re-layouts  35.9 us (14%)
  starting transfers between devices  22.8 us (9%)
  blocking collectives  7.96 us (3%)
    all_to_all x2, waiting for transfers between devices, body(): lax.all_to_all(picked, ('lo', 'tm'), split_axis=0, concat_axis=0, tiled=T...  53.9 us
    pallas_call x6, Pallas kernels, iterate(): pl.pallas_call(functools.partial(iterate_kernel, len(images), len(volts))...  46.4 us
    ppermute x1, waiting for transfers between devices, body(): far_windows = lax.ppermute(own_windows, 'hi', SWAP)  37 us
    pallas_call x4, local copies, waits for them, and re-layouts, raw_power(): pl.pallas_call(raw_kernel, out_shape=jax.ShapeDtypeStruct((1, 1, width),...  16.1 us
    pallas_call x4, Pallas kernels, raw_power(): pl.pallas_call(raw_kernel, out_shape=jax.ShapeDtypeStruct((1, 1, width),...  16 us
    pallas_call x1, Pallas kernels, nulled_power(): pl.pallas_call(functools.partial(null_kernel, len(volts)), out_shape=jax....  13.8 us
    pallas_call x1, Pallas kernels, steering(): pl.pallas_call(steer_kernel, out_shape=jax.ShapeDtypeStruct((channels, 2,...  13.1 us
    all_to_all x2, starting transfers between devices, body(): lax.all_to_all(picked, ('lo', 'tm'), split_axis=0, concat_axis=0, tiled=T...  11.9 us
  transfers between devices with their start and end apart: 10, of which 7 were waited for; matrix products, arithmetic and copies ran while one was open for 9% of the time, Pallas kernels for 11%

profile of v2, /device:TPU:0, one launch (start us, length us, event | category | flops | bytes accessed | tf_op | source)
XLA Modules:
  0.0 260.4 jit_solution(15842793081565940861)
XLA Ops:
  0.0 5.3 %fusion.3 = (bf16[2,1,16,2,64,512]{5,4,3,2,1,0:T(8,128)(2,1)}, bf16[2,1,16,2,64,512]{5,4,3,2,1,0:T(8,128)(2,1)S(1)}) fusion(bf16[2,2,16,2,64,512]{5,4,3,2,1,0:T(8,128)(2,1)} %bitcast.33), kind=kLoop, calls=%fused_computation.31 | loop fusion | bytes 16777216 | tf_op jit(solution)/shard_map/slice | solution.py:285
  7.8 6.4 %all-to-all-start = ((bf16[16,2,2,64,512]{4,3,2,1,0:T(8,128)(2,1)}), bf16[16,2,2,64,512]{4,3,2,1,0:T(8,128)(2,1)}, u32[]{:S(2)}, u32[]{:S(2)}) async-start(bf16[16,2,2,64,512]{4,3,2,1,0:T(8,128)(2,1)} %bitcast.32), calls=%async_computation | async-start | bytes 8388608 | tf_op jit(solution)/shard_map/all_to_all | solution.py:286
  14.2 4.6 %copy.30 = bf16[2,1,16,2,64,512]{5,4,3,0,2,1:T(8,128)(2,1)} copy(bf16[2,1,16,2,64,512]{5,4,3,2,1,0:T(8,128)(2,1)} %get-tuple-element.5) | data formatting | bytes 8388608
  18.8 53.9 %all-to-all-done.refs_1_.refs_2_.refs_0_ = bf16[16,2,2,64,512]{4,3,2,1,0:T(8,128)(2,1)} async-done(((bf16[16,2,2,64,512]{4,3,2,1,0:T(8,128)(2,1)}), bf16[16,2,2,64,512]{4,3,2,1,0:T(8,128)(2,1)}, u32[]{:S(2)}, u32[]{:S(2)}) %all-to-all-start) | async-done | bytes 4194336 | tf_op jit(solution)/shard_map/all_to_all | solution.py:286
  72.6 5.5 %all-to-all-start.1 = ((bf16[16,2,2,64,512]{4,3,2,1,0:T(8,128)(2,1)}), bf16[16,2,2,64,512]{4,3,2,1,0:T(8,128)(2,1)}, u32[]{:S(2)}, u32[]{:S(2)}) async-start(bf16[16,2,2,64,512]{4,3,2,1,0:T(8,128)(2,1)} %bitcast.31), calls=%async_computation.1 | async-start | bytes 8388608 | tf_op jit(solution)/shard_map/all_to_all | solution.py:286
  84.9 13.1 %steering.1.steer_ref = bf16[4,2,512,1024]{3,2,1,0:T(8,128)(2,1)S(1)} custom-call(f32[4]{0:T(128)S(1)} %fusion.2.freq_ref, f32[512,2]{1,0:T(8,128)S(1)} %bitcast.29, f32[2,1024]{1,0:T(2,128)S(1)} %select_bitcast_fusion.toward_ref), custom_call_target="tpu_custom_call" | custom-call | flops 83886080 | bytes 8388608 | tf_op jit(solution)/shard_map/steering/pallas_call | solution.py:248
  101.2 37.0 %collective-permute-done = s32[2,2]{1,0:T(2,128)S(1)} collective-permute-done((s32[2,2]{1,0:T(2,128)S(1)}, s32[2,2]{1,0:T(2,128)S(1)}, u32[]{:S(2)}, u32[]{:S(2)}) %collective-permute-start) | collective-permute-done | bytes 48 | tf_op jit(solution)/shard_map/ppermute | solution.py:291
  139.4 7.8 %iterate.6.refs_0_ = bf16[4,16,512]{2,1,0:T(8,128)(2,1)S(1)} custom-call(s32[4,2]{1,0:T(4,128)S(1)} %pad_add_fusion.win_ref, s32[1]{0:T(128)} %bitcast.start_ref, f32[4,16,512]{2,1,0:T(8,128)S(1)} %pad_maximum_fusion.refs_0_, bf16[16,2,2,64,512]{4,3,2,1,0:T(8,128)(2,1)} %all-to-all-done.refs_1_.refs_2_.refs_0_, ...), custom_call_target="tpu_custom_call" | custom-call | flops 268435456 | bytes 8388608 | tf_op jit(solution)/shard_map/iterate/pallas_call | solution.py:94
  150.6 4.0 %raw_power.8.refs_4_ = f32[1,1,512]{2,1,0:T(1,128)S(1)} custom-call(bf16[16,2,2,64,512]{4,3,2,1,0:T(8,128)(2,1)} %all-to-all-done.1.refs_2_.volt_ref.refs_3_.refs_1_, bf16[4,2,512,1024]{3,2,1,0:T(8,128)(2,1)S(1)} %copy-done.2, bf16[4,16,512]{2,1,0:T(8,128)(2,1)S(1)} %iterate.6.refs_0_), custom_call_target="tpu_custom_call" | custom-call | flops 2147483648 | bytes 1048576 | tf_op jit(solution)/shard_map/raw_power/pallas_call | solution.py:118
  154.6 4.0 %raw_power.15 = f32[8,1,512]{2,1,0:T(1,128)S(1)} fusion(f32[8,1,512]{2,1,0:T(1,128)S(1)} %custom-call, bf16[16,2,2,64,512]{4,3,2,1,0:T(8,128)(2,1)} %all-to-all-done.refs_1_.refs_2_.refs_0_, bf16[4,2,512,1024]{3,2,1,0:T(8,128)(2,1)S(1)} %copy-done.2), kind=kCustom, calls=%fused_computation.15 | custom fusion | bytes 12584960 | tf_op jit(solution)/shard_map/raw_power/pallas_call | solution.py:118
  158.6 4.0 %raw_power.14 = f32[8,1,512]{2,1,0:T(1,128)S(1)} fusion(f32[8,1,512]{2,1,0:T(1,128)S(1)} %raw_power.15, bf16[16,2,2,64,512]{4,3,2,1,0:T(8,128)(2,1)} %all-to-all-done.refs_1_.refs_2_.refs_0_, bf16[4,2,512,1024]{3,2,1,0:T(8,128)(2,1)S(1)} %copy-done.2), kind=kCustom, calls=%fused_computation.14 | custom fusion | bytes 12584960 | tf_op jit(solution)/shard_map/raw_power/pallas_call | solution.py:118
  162.7 4.0 %raw_power.13 = f32[8,1,512]{2,1,0:T(1,128)S(1)} fusion(f32[8,1,512]{2,1,0:T(1,128)S(1)} %raw_power.14, bf16[16,2,2,64,512]{4,3,2,1,0:T(8,128)(2,1)} %all-to-all-done.refs_1_.refs_2_.refs_0_, bf16[4,2,512,1024]{3,2,1,0:T(8,128)(2,1)S(1)} %copy-done.2), kind=kCustom, calls=%fused_computation.13 | custom fusion | bytes 12584960 | tf_op jit(solution)/shard_map/raw_power/pallas_call | solution.py:118
  166.7 4.0 %raw_power.12 = f32[8,1,512]{2,1,0:T(1,128)S(1)} fusion(f32[8,1,512]{2,1,0:T(1,128)S(1)} %raw_power.13, bf16[16,2,2,64,512]{4,3,2,1,0:T(8,128)(2,1)} %all-to-all-done.refs_1_.refs_2_.refs_0_, bf16[4,2,512,1024]{3,2,1,0:T(8,128)(2,1)S(1)} %copy-done.2), kind=kCustom, calls=%fused_computation.12 | custom fusion | bytes 12584960 | tf_op jit(solution)/shard_map/raw_power/pallas_call | solution.py:118
  170.7 7.8 %iterate.7.refs_0_ = bf16[4,16,512]{2,1,0:T(8,128)(2,1)S(1)} custom-call(s32[4,2]{1,0:T(4,128)S(1)} %pad_add_fusion.win_ref, s32[1]{0:T(128)} %bitcast.start_ref, bf16[4,16,512]{2,1,0:T(8,128)(2,1)S(1)} %iterate.6.refs_0_, bf16[4,16,512]{2,1,0:T(8,128)(2,1)S(1)} %collective-permute-done.2.refs_1_, ...), custom_call_target="tpu_custom_call" | custom-call | flops 268435456 | bytes 8388608 | tf_op jit(solution)/shard_map/iterate/pallas_call | solution.py:94
  183.8 7.6 %iterate.8.refs_0_ = bf16[4,16,512]{2,1,0:T(8,128)(2,1)S(1)} custom-call(s32[4,2]{1,0:T(4,128)S(1)} %pad_add_fusion.win_ref, s32[1]{0:T(128)} %bitcast.start_ref, bf16[4,16,512]{2,1,0:T(8,128)(2,1)S(1)} %iterate.7.refs_0_, bf16[4,16,512]{2,1,0:T(8,128)(2,1)S(1)} %collective-permute-done.3.refs_1_, ...), custom_call_target="tpu_custom_call" | custom-call | flops 268435456 | bytes 8388608 | tf_op jit(solution)/shard_map/iterate/pallas_call | solution.py:94
  193.1 4.0 %raw_power.10.refs_4_ = f32[1,1,512]{2,1,0:T(1,128)S(1)} custom-call(bf16[16,2,2,64,512]{4,3,2,1,0:T(8,128)(2,1)} %all-to-all-done.1.refs_2_.volt_ref.refs_3_.refs_1_, bf16[4,2,512,1024]{3,2,1,0:T(8,128)(2,1)S(1)} %copy-done.2, bf16[4,16,512]{2,1,0:T(8,128)(2,1)S(1)} %iterate.8.refs_0_), custom_call_target="tpu_custom_call" | custom-call | flops 2147483648 | bytes 1048576 | tf_op jit(solution)/shard_map/raw_power/pallas_call | solution.py:118
  197.2 7.6 %iterate.9.refs_0_ = bf16[4,16,512]{2,1,0:T(8,128)(2,1)S(1)} custom-call(s32[4,2]{1,0:T(4,128)S(1)} %pad_add_fusion.win_ref, s32[1]{0:T(128)} %bitcast.start_ref, bf16[4,16,512]{2,1,0:T(8,128)(2,1)S(1)} %iterate.8.refs_0_, bf16[4,16,512]{2,1,0:T(8,128)(2,1)S(1)} %collective-permute-done.4.refs_1_, ...), custom_call_target="tpu_custom_call" | custom-call | flops 268435456 | bytes 8388608 | tf_op jit(solution)/shard_map/iterate/pallas_call | solution.py:94
  206.0 4.0 %raw_power.11.refs_4_ = f32[1,1,512]{2,1,0:T(1,128)S(1)} custom-call(bf16[16,2,2,64,512]{4,3,2,1,0:T(8,128)(2,1)} %all-to-all-done.1.refs_2_.volt_ref.refs_3_.refs_1_, bf16[4,2,512,1024]{3,2,1,0:T(8,128)(2,1)S(1)} %copy-done.2, bf16[4,16,512]{2,1,0:T(8,128)(2,1)S(1)} %iterate.9.refs_0_), custom_call_target="tpu_custom_call" | custom-call | flops 2147483648 | bytes 1048576 | tf_op jit(solution)/shard_map/raw_power/pallas_call | solution.py:118
  210.7 7.9 %iterate.10.refs_0_ = bf16[4,16,512]{2,1,0:T(8,128)(2,1)S(1)} custom-call(s32[4,2]{1,0:T(4,128)S(1)} %pad_add_fusion.win_ref, s32[1]{0:T(128)} %bitcast.start_ref, bf16[4,16,512]{2,1,0:T(8,128)(2,1)S(1)} %iterate.9.refs_0_, bf16[4,16,512]{2,1,0:T(8,128)(2,1)S(1)} %collective-permute-done.5.refs_1_, ...), custom_call_target="tpu_custom_call" | custom-call | flops 268435456 | bytes 8388608 | tf_op jit(solution)/shard_map/iterate/pallas_call | solution.py:94
  219.7 4.8 %collective-permute-done.6.refs_1_ = bf16[4,16,512]{2,1,0:T(8,128)(2,1)S(1)} collective-permute-done((bf16[4,16,512]{2,1,0:T(8,128)(2,1)S(1)}, bf16[4,16,512]{2,1,0:T(8,128)(2,1)S(1)}, u32[]{:S(2)}, u32[]{:S(2)}) %collective-permute-start.6) | collective-permute-done | bytes 65568 | tf_op jit(solution)/shard_map/ppermute | solution.py:319
  224.4 7.6 %iterate.11.own_ref = bf16[4,16,512]{2,1,0:T(8,128)(2,1)S(1)} custom-call(s32[4,2]{1,0:T(4,128)S(1)} %pad_add_fusion.win_ref, s32[1]{0:T(128)} %bitcast.start_ref, bf16[4,16,512]{2,1,0:T(8,128)(2,1)S(1)} %iterate.10.refs_0_, bf16[4,16,512]{2,1,0:T(8,128)(2,1)S(1)} %collective-permute-done.6.refs_1_, ...), custom_call_target="tpu_custom_call" | custom-call | flops 268435456 | bytes 8388608 | tf_op jit(solution)/shard_map/iterate/pallas_call | solution.py:94
  232.6 4.8 %collective-permute-done.7.other_ref = bf16[4,16,512]{2,1,0:T(8,128)(2,1)S(1)} collective-permute-done((bf16[4,16,512]{2,1,0:T(8,128)(2,1)S(1)}, bf16[4,16,512]{2,1,0:T(8,128)(2,1)S(1)}, u32[]{:S(2)}, u32[]{:S(2)}) %collective-permute-start.7) | collective-permute-done | bytes 65568 | tf_op jit(solution)/shard_map/ppermute | solution.py:319
  237.4 13.8 %nulled_power.1 = f32[4,1,1024]{2,1,0:T(1,128)S(1)} custom-call(bf16[4,16,512]{2,1,0:T(8,128)(2,1)S(1)} %iterate.11.own_ref, bf16[4,16,512]{2,1,0:T(8,128)(2,1)S(1)} %collective-permute-done.7.other_ref, f32[4,1,1024]{2,1,0:T(1,128)S(1)} %bitcast.30, bf16[4,2,512,1024]{3,2,1,0:T(8,128)(2,1)} %copy-done.1, ...), custom_call_target="tpu_custom_call" | custom-call | flops 671088640 | bytes 16777216 | tf_op jit(solution)/shard_map/nulled_power/pallas_call | solution.py:192
  251.3 8.0 %all_to_all.15 = f32[4,2,512]{2,1,0:T(2,128)S(1)} all-to-all(f32[4,2,512]{2,1,0:T(2,128)S(1)} %bitcast.34), channel_id=1, replica_groups=mesh['hi'=2,'lo'=8,'tm'=2] {'hi','tm'}, dimensions={0} | all-to-all | bytes 32768 | tf_op jit(solution)/shard_map/all_to_all | solution.py:332
  (56 shorter events, 28.1 us)
Async XLA Ops:
  0.0 80.9 %copy-start = (f32[2,4,8,512]{3,2,1,0:T(8,128)S(1)}, f32[2,4,8,512]{3,2,1,0:T(8,128)}, u32[]{:S(2)}) copy-start(f32[2,4,8,512]{3,2,1,0:T(8,128)} %param.8) | copy-start | bytes 393220
  7.8 64.9 %all-to-all-start = ((bf16[16,2,2,64,512]{4,3,2,1,0:T(8,128)(2,1)}), bf16[16,2,2,64,512]{4,3,2,1,0:T(8,128)(2,1)}, u32[]{:S(2)}, u32[]{:S(2)}) async-start(bf16[16,2,2,64,512]{4,3,2,1,0:T(8,128)(2,1)} %bitcast.32), calls=%async_computation | async-start | bytes 8388608 | tf_op jit(solution)/shard_map/all_to_all | solution.py:286
  72.6 5.5 %copy-start.6 = (s32[4,2]{0,1:T(2,128)S(1)}, s32[4,2]{0,1:T(2,128)}, u32[]{:S(2)}) copy-start(s32[4,2]{0,1:T(2,128)} %param.7) | copy-start | bytes 100
  72.6 8.7 %copy-start.5 = (f32[2,512]{1,0:T(2,128)S(1)}, f32[2,512]{1,0:T(2,128)}, u32[]{:S(2)}) copy-start(f32[2,512]{1,0:T(2,128)} %param.9) | copy-start | bytes 12292
  72.6 8.9 %copy-start.4 = (f32[2,1024]{1,0:T(2,128)S(1)}, f32[2,1024]{1,0:T(2,128)}, u32[]{:S(2)}) copy-start(f32[2,1024]{1,0:T(2,128)} %param.10) | copy-start | bytes 24580
  72.6 9.1 %copy-start.3 = (s32[1024]{0:T(1024)S(1)}, s32[1024]{0:T(1024)}, u32[]{:S(2)}) copy-start(s32[1024]{0:T(1024)} %param.11) | copy-start | bytes 12292
  72.6 66.8 %all-to-all-start.1 = ((bf16[16,2,2,64,512]{4,3,2,1,0:T(8,128)(2,1)}), bf16[16,2,2,64,512]{4,3,2,1,0:T(8,128)(2,1)}, u32[]{:S(2)}, u32[]{:S(2)}) async-start(bf16[16,2,2,64,512]{4,3,2,1,0:T(8,128)(2,1)} %bitcast.31), calls=%async_computation.1 | async-start | bytes 8388608 | tf_op jit(solution)/shard_map/all_to_all | solution.py:286
  78.3 59.9 %collective-permute-start = (s32[2,2]{1,0:T(2,128)S(1)}, s32[2,2]{1,0:T(2,128)S(1)}, u32[]{:S(2)}, u32[]{:S(2)}) collective-permute-start(s32[2,2]{1,0:T(2,128)S(1)} %copy.20), channel_id=1, source_target_pairs={{0,16},{16,0},{1,17},{17,1},{2,18},{18,2},{3,19},{19,3},{4,20},{20... | collective-permute-start | bytes 56 | tf_op jit(solution)/shard_map/ppermute | solution.py:291
  80.9 58.5 %collective-permute-start.1 = (f32[2,16,512]{2,1,0:T(8,128)S(1)}, f32[2,16,512]{2,1,0:T(8,128)S(1)}, u32[]{:S(2)}, u32[]{:S(2)}) collective-permute-start(f32[2,16,512]{2,1,0:T(8,128)S(1)} %copy_bitcast_fusion.2), channel_id=1, source_target_pairs={{0,16},{16,0},{1,17},{17,1},{2,18},{18,2},{3,19},{19,3},{4,20},{20... | collective-permute-start | bytes 196616 | tf_op jit(solution)/shard_map/ppermute | solution.py:292
  98.0 3.2 %copy-start.1 = (bf16[4,2,512,1024]{3,2,1,0:T(8,128)(2,1)}, bf16[4,2,512,1024]{3,2,1,0:T(8,128)(2,1)S(1)}, u32[]{:S(2)}) copy-start(bf16[4,2,512,1024]{3,2,1,0:T(8,128)(2,1)S(1)} %steering.1.steer_ref) | copy-start | bytes 25165828
  139.4 11.2 %copy-start.2 = (bf16[4,2,512,1024]{3,2,1,0:T(8,128)(2,1)S(1)}, bf16[4,2,512,1024]{3,2,1,0:T(8,128)(2,1)}, u32[]{:S(2)}) copy-start(bf16[4,2,512,1024]{3,2,1,0:T(8,128)(2,1)} %copy-done.1) | copy-start | bytes 25165828
  147.2 23.5 %collective-permute-start.2 = (bf16[4,16,512]{2,1,0:T(8,128)(2,1)S(1)}, bf16[4,16,512]{2,1,0:T(8,128)(2,1)S(1)}, u32[]{:S(2)}, u32[]{:S(2)}) collective-permute-start(bf16[4,16,512]{2,1,0:T(8,128)(2,1)S(1)} %iterate.6.refs_0_), channel_id=1, source_target_pairs={{0,16},{16,0},{1,17},{17,1},{2,18},{18,2},{3,19},{19,3},{4,20},{20... | collective-permute-start | bytes 196616 | tf_op jit(solution)/shard_map/ppermute | solution.py:319
  178.5 5.2 %collective-permute-start.3 = (bf16[4,16,512]{2,1,0:T(8,128)(2,1)S(1)}, bf16[4,16,512]{2,1,0:T(8,128)(2,1)S(1)}, u32[]{:S(2)}, u32[]{:S(2)}) collective-permute-start(bf16[4,16,512]{2,1,0:T(8,128)(2,1)S(1)} %iterate.7.refs_0_), channel_id=1, source_target_pairs={{0,16},{16,0},{1,17},{17,1},{2,18},{18,2},{3,19},{19,3},{4,20},{20... | collective-permute-start | bytes 196616 | tf_op jit(solution)/shard_map/ppermute | solution.py:319
  191.4 5.7 %collective-permute-start.4 = (bf16[4,16,512]{2,1,0:T(8,128)(2,1)S(1)}, bf16[4,16,512]{2,1,0:T(8,128)(2,1)S(1)}, u32[]{:S(2)}, u32[]{:S(2)}) collective-permute-start(bf16[4,16,512]{2,1,0:T(8,128)(2,1)S(1)} %iterate.8.refs_0_), channel_id=1, source_target_pairs={{0,16},{16,0},{1,17},{17,1},{2,18},{18,2},{3,19},{19,3},{4,20},{20... | collective-permute-start | bytes 196616 | tf_op jit(solution)/shard_map/ppermute | solution.py:319
  204.8 5.9 %collective-permute-start.5 = (bf16[4,16,512]{2,1,0:T(8,128)(2,1)S(1)}, bf16[4,16,512]{2,1,0:T(8,128)(2,1)S(1)}, u32[]{:S(2)}, u32[]{:S(2)}) collective-permute-start(bf16[4,16,512]{2,1,0:T(8,128)(2,1)S(1)} %iterate.9.refs_0_), channel_id=1, source_target_pairs={{0,16},{16,0},{1,17},{17,1},{2,18},{18,2},{3,19},{19,3},{4,20},{20... | collective-permute-start | bytes 196616 | tf_op jit(solution)/shard_map/ppermute | solution.py:319
  218.6 5.9 %collective-permute-start.6 = (bf16[4,16,512]{2,1,0:T(8,128)(2,1)S(1)}, bf16[4,16,512]{2,1,0:T(8,128)(2,1)S(1)}, u32[]{:S(2)}, u32[]{:S(2)}) collective-permute-start(bf16[4,16,512]{2,1,0:T(8,128)(2,1)S(1)} %iterate.10.refs_0_), channel_id=1, source_target_pairs={{0,16},{16,0},{1,17},{17,1},{2,18},{18,2},{3,19},{19,3},{4,20},{20... | collective-permute-start | bytes 196616 | tf_op jit(solution)/shard_map/ppermute | solution.py:319
  232.1 5.3 %collective-permute-start.7 = (bf16[4,16,512]{2,1,0:T(8,128)(2,1)S(1)}, bf16[4,16,512]{2,1,0:T(8,128)(2,1)S(1)}, u32[]{:S(2)}, u32[]{:S(2)}) collective-permute-start(bf16[4,16,512]{2,1,0:T(8,128)(2,1)S(1)} %iterate.11.own_ref), channel_id=1, source_target_pairs={{0,16},{16,0},{1,17},{17,1},{2,18},{18,2},{3,19},{19,3},{4,20},{20... | collective-permute-start | bytes 196616 | tf_op jit(solution)/shard_map/ppermute | solution.py:319
